TPU v7x, 128 devices: a whole 4x4x4 slice. The times are simulated.
128 devices in a mesh: grp: 4 (over y), blk: 32 (over z, x, core).
Axes of the slice: x: 4, y: 4, z: 4, core: 2. Of those that a mesh axis runs over, the one named last changes fastest.
Arguments:
- displacement: float32 [3, 125, 131072], P(None, None, ('grp', 'blk')), may hold values from -0.4 to 0.4, as said below
- velocity: float32 [3, 125, 131072], P(None, None, ('grp', 'blk')), may hold values from -4 to 4, as said below
- lame: float32 [2, 131072], P(None, ('grp', 'blk')), may hold values from 0.5 to 2
- fault_props: float32 [7, 25, 16384], P(None, None, ('grp', 'blk')), may hold values from -4 to 6, as said below
- fault_slots: int32 [16384], P(('grp', 'blk')), may hold values from 0 to 127, as said below
Outputs:
- velocity_new: float32 [3, 125, 131072], P(None, None, ('grp', 'blk'))
- slip_rate: float32 [25, 16384], P(None, ('grp', 'blk'))
- theta_new: float32 [25, 16384], P(None, ('grp', 'blk'))
Inputs may be any that keep to these rules, and one draw needn't show every extreme that they name: `fault_slots`: each device's 128 entries are a permutation of 0 to 127. `displacement`: entries at one node shared by several elements are equal, except across the fault plane. `velocity`: entries at one node shared by several elements are equal, except across the fault plane. `fault_props`: Rows: state in 0.3 to 3, a in 0.3 to 0.6, b in 0.1 to 0.4, slip distance in 0.5 to 1.5, two prestresses in -4 to 4, normal stress in 2 to 6; entries of one fault node shared by neighbouring faces are equal.
All inputs are finite; a program needn't handle non-finite values.
Results may differ from a plain program's by a relative error of at most 0.0001.
Values sent between devices are 32-bit elements; how exact they have to be, the bound alone decides.
No kernel may reach another device: no remote copies, remote signals or barrier semaphores. Data moves between devices by JAX's collectives and lax.ppermute only.
A program may use at most 64 MiB of HBM per device.

v0:
```python
import jax
import jax.numpy as jnp
import numpy as np
from jax import lax
from jax.experimental import pallas as pl
from jax.experimental.pallas import tpu as pltpu
from jax.sharding import PartitionSpec as P

NEWTON = 3
GLL_POINTS = np.array([-1.0, -np.sqrt(3.0 / 7.0), 0.0, np.sqrt(3.0 / 7.0), 1.0])
GLL_WEIGHTS = np.array([0.1, 49.0 / 90.0, 32.0 / 45.0, 49.0 / 90.0, 0.1])
DT = 0.01
W_END = 0.1
ETA = W_END / (2.0 * DT)
CORRECTION = DT / W_END
FRICTION_REF = 0.6
TRACTION_FLOOR = 1.0
N_GRP = 4
N_BLK = 32
F32 = jnp.float32
HIGHEST = lax.Precision.HIGHEST


def derivative_table():
    x = GLL_POINTS
    bary = [1.0 / np.prod([x[c] - x[o] for o in range(5) if o != c]) for c in range(5)]
    table = np.zeros((5, 5))
    for r in range(5):
        for c in range(5):
            if r != c:
                table[r, c] = bary[c] / bary[r] / (x[r] - x[c])
        table[r, r] = -np.sum(table[r])
    return table


D_TABLE = derivative_table()
M_TABLE = -DT * D_TABLE.T * GLL_WEIGHTS[None, :] / GLL_WEIGHTS[:, None]


def line(table, u):
    e0, e1 = u[0] + u[4], u[1] + u[3]
    o0, o1 = u[0] - u[4], u[1] - u[3]
    out = [None] * 5
    for i in range(2):
        even = (
            float((table[i, 0] + table[i, 4]) / 2) * e0
            + float((table[i, 1] + table[i, 3]) / 2) * e1
            + float(table[i, 2]) * u[2]
        )
        odd = (
            float((table[i, 0] - table[i, 4]) / 2) * o0
            + float((table[i, 1] - table[i, 3]) / 2) * o1
        )
        out[i] = odd + even
        out[4 - i] = odd - even
    out[2] = float(table[2, 0]) * o0 + float(table[2, 1]) * o1
    return out


def node(p, q, r):
    return 25 * p + 5 * q + r


def roll(x, shift, axis):
    shift = shift % x.shape[axis]
    return x if shift == 0 else pltpu.roll(x, shift, axis)


def row(ref, c, n):
    return ref[c, n, :].reshape(8, 128)


def tile_iota():
    lane = lax.broadcasted_iota(jnp.int32, (8, 128), 1)
    sub = lax.broadcasted_iota(jnp.int32, (8, 128), 0)
    return lane, sub, lane // 32, lane % 32, sub // 2


def inverse_sinh(value):
    return jnp.log(value + jnp.sqrt(1.0 + value * value))


def own_scales(grp, blk):
    half = lambda has: jnp.where(has, 0.5, 1.0).astype(F32)
    return half(blk > 0), half(blk < N_BLK - 1), half(grp > 0), half(grp < N_GRP - 1)


def slot_hot(slots):
    r = lax.broadcasted_iota(jnp.int32, (128, 128), 0)
    face = (r % 8) * 16 + (r // 8 % 4) * 4 + r // 32
    return (jnp.broadcast_to(slots, (128, 128)) == face).astype(F32)


def fault_jump(get):
    return get(0) - roll(roll(get(4), 32, 1), 1, 0)


def force_kernel(
    disp, vel, lame, props, slots,
    f_out, xe_out, xo_out, ze_out, zo_out, abuf,
    gx, gy, sj, xs, sc,
):
    grp = lax.axis_index("grp")
    blk = lax.axis_index("blk")
    lane, sub, jl, k, i_el = tile_iota()
    lam = lame[0, :].reshape(8, 128)
    mu = lame[1, :].reshape(8, 128)
    mu2 = mu + mu
    x0, x4, z0, z4 = own_scales(grp, blk)

    for c in range(3):
        for r in range(5):
            u = [[row(disp, c, node(p, q, r)) for q in range(5)] for p in range(5)]
            for q in range(5):
                out = line(D_TABLE, [u[p][q] for p in range(5)])
                for p in range(5):
                    gx[c, node(p, q, r)] = out[p]
            for p in range(5):
                out = line(D_TABLE, u[p])
                for q in range(5):
                    gy[c, node(p, q, r)] = out[q]

    for p in range(5):
        for q in range(5):
            gz = [
                line(D_TABLE, [row(disp, c, node(p, q, r)) for r in range(5)]) for c in range(3)
            ]
            sz = [[None] * 5 for _ in range(3)]
            for r in range(5):
                n = node(p, q, r)
                g0 = [gx[c, n] for c in range(3)]
                g1 = [gy[c, n] for c in range(3)]
                g2 = [gz[c][r] for c in range(3)]
                spread = lam * (g0[0] + g1[1] + g2[2])
                s01 = mu * (g0[1] + g1[0])
                s02 = mu * (g0[2] + g2[0])
                s12 = mu * (g1[2] + g2[1])
                gx[0, n] = spread + mu2 * g0[0]
                gx[1, n] = s01
                gx[2, n] = s02
                gy[1, n] = spread + mu2 * g1[1]
                gy[2, n] = s12
                sz[0][r], sz[1][r], sz[2][r] = s02, s12, spread + mu2 * g2[2]
            for c in range(3):
                out = line(M_TABLE, sz[c])
                for r in range(5):
                    f_out[c, node(p, q, r)] = out[r]

    y4_in, y0_in = jl < 3, jl > 0
    x4_in, x0_in = i_el < 3, i_el > 0
    for c in range(3):
        for r in range(5):
            f = [[f_out[c, node(p, q, r)] for q in range(5)] for p in range(5)]
            for p in range(5):
                if c == 0:
                    s = [gx[1, node(p, q, r)] for q in range(5)]
                else:
                    s = [gy[c, node(p, q, r)] for q in range(5)]
                out = line(M_TABLE, s)
                for q in range(5):
                    f[p][q] = f[p][q] + out[q]
            for q in range(5):
                out = line(M_TABLE, [gx[c, node(p, q, r)] for p in range(5)])
                for p in range(5):
                    f[p][q] = f[p][q] + out[p]
            for p in range(5):
                avg = 0.5 * (f[p][4] + roll(f[p][0], -32, 1))
                f[p][0] = jnp.where(y0_in, roll(avg, 32, 1), f[p][0])
                f[p][4] = jnp.where(y4_in, avg, f[p][4])
            for q in range(5):
                avg = 0.5 * (f[4][q] + roll(f[0][q], -2, 0))
                f[0][q] = jnp.where(x0_in, roll(avg, 2, 0), f[0][q] * x0)
                f[4][q] = jnp.where(x4_in, avg, f[4][q] * x4)
            for p in range(5):
                for q in range(5):
                    f_out[c, node(p, q, r)] = f[p][q]

    z4_in, z0_in = k < 31, k > 0
    zero = jnp.zeros((8, 128), F32)
    zlo, zhi = [zero] * 3, [zero] * 3
    for c in range(3):
        for p in range(5):
            for q in range(5):
                n0, n4 = node(p, q, 0), node(p, q, 4)
                a0, a4 = f_out[c, n0], f_out[c, n4]
                avg = 0.5 * (a4 + roll(a0, -1, 1))
                a0 = jnp.where(z0_in, roll(avg, 1, 1), a0 * z0)
                a4 = jnp.where(z4_in, avg, a4 * z4)
                f_out[c, n0] = a0
                f_out[c, n4] = a4
                m = c * 25 + p * 5 + q
                at = k == m % 32
                zlo[m // 32] = jnp.where(at, roll(a0, m % 32, 1), zlo[m // 32])
                zhi[m // 32] = jnp.where(at, roll(a4, m % 32 - 31, 1), zhi[m // 32])
    z_even = grp % 2 == 0
    for g in range(3):
        ze_out[g] = jnp.where(z_even, zhi[g], zlo[g])
        zo_out[g] = jnp.where(z_even, zlo[g], zhi[g])

    x_even = blk % 2 == 0
    for c in range(3):
        for q in range(5):
            for r in range(5):
                m = c * 25 + q * 5 + r
                lo = f_out[c, node(0, q, r)]
                hi = roll(f_out[c, node(4, q, r)], 2, 0)
                xe_out[m] = jnp.where(x_even, hi, lo)[0:2]
                xo_out[m] = jnp.where(x_even, lo, hi)[0:2]

    for t in range(128):
        abuf[pl.ds(8 * t, 8), :] = zero
    own_x = {0: jnp.where(x0_in, 1.0, x0), 4: jnp.where(x4_in, 1.0, x4)}
    own_z = {0: jnp.where(z0_in, 1.0, z0), 4: jnp.where(z4_in, 1.0, z4)}
    for p in range(5):
        for c in range(3):
            jump = [None] * 5
            for r in range(5):
                own = None
                for part in (own_x.get(p), own_z.get(r)):
                    if part is not None:
                        own = part if own is None else own * part

                def side(q, own=own, r=r):
                    v = row(vel, c, node(p, q, r))
                    return f_out[c, node(p, q, r)] + (v if own is None else v * own)

                jump[r] = fault_jump(side)
                sj[pl.ds(8 * (p * 24 + c * 8 + r), 8), :] = jump[r]
            extra = jnp.where(k == 0, roll(jump[4], -31, 1), 0.0)
            extra = jnp.where(k == 31, roll(jump[0], 31, 1), extra)
            sj[pl.ds(8 * (p * 24 + c * 8 + 5), 8), :] = extra
            sj[pl.ds(8 * (p * 24 + c * 8 + 6), 8), :] = zero
            sj[pl.ds(8 * (p * 24 + c * 8 + 7), 8), :] = zero
    for t in range(120, 128):
        sj[pl.ds(8 * t, 8), :] = zero
    lane_big = lax.broadcasted_iota(jnp.int32, (128, 128), 1)
    y = None
    for i in range(4):
        part = roll(sj[pl.ds(2 * i + 1, 128, stride=8), :], 32 * i, 1)
        y = part if y is None else jnp.where(lane_big // 32 == i, part, y)
    yt = y.T
    dest = blk // 8

    def put_jump(d):
        for i in range(4):
            abuf[pl.ds(d * 256 + i, 32, stride=8), :] = yt[32 * i : 32 * i + 32]

    put_jump(dest)

    @pl.when((blk % 8 == 7) & (dest < N_GRP - 1))
    def _():
        put_jump(dest + 1)

    @pl.when((blk % 8 == 0) & (dest > 0))
    def _():
        put_jump(dest - 1)

    xs[...] = jnp.zeros((128, 128), F32)
    theta, a, b, length = props[0], props[1], props[2], props[3]
    xs[0:25] = props[4]
    xs[32:57] = props[5]
    xs[64:89] = 0.5 * jnp.exp((FRICTION_REF + b * jnp.log(theta / length)) / a)
    xs[96:121] = props[6] * a
    packed = lax.dot_general(
        slot_hot(slots[...]), xs[...], (((1,), (1,)), ((), ())),
        precision=HIGHEST, preferred_element_type=F32,
    )
    for u in range(4):
        for i in range(4):
            t = u * 4 + i
            abuf[pl.ds(u * 256 + grp * 64 + 4 + i, 8, stride=8), :] = packed[8 * t : 8 * t + 8]

    sc[pl.ds(120, 8), :] = zero
    for q in range(5):
        for c in range(3):
            low = jnp.where(k < 16, f_out[c, node(0, q, 0)], f_out[c, node(0, q, 4)])
            high = jnp.where(k < 16, f_out[c, node(4, q, 0)], f_out[c, node(4, q, 4)])
            sc[pl.ds(q * 24 + c * 8, 8), :] = jnp.where(sub < 4, low, high)
    sc[...] = sc[...].T
    at_edge = lax.broadcasted_iota(jnp.int32, (4, 128), 1) % 8 >= 6
    for dg in (-1, 1):
        for db in (-1, 1):
            ok = (grp + dg >= 0) & (grp + dg < N_GRP) & (blk + db >= 0) & (blk + db < N_BLK)
            value = sc[pl.ds(31 if dg > 0 else 0, 4, stride=32), :]
            if db < 0:
                value = roll(value, 6, 1)

            @pl.when(ok)
            def _(value=value, dg=dg, db=db):
                at = 8 * ((grp + dg) * N_BLK + blk + db)
                abuf[pl.ds(at, 4), :] = jnp.where(at_edge, value, abuf[pl.ds(at, 4), :])


def solve(trial_x, trial_z, scale_c, sigma_a):
    trial_norm = jnp.sqrt(trial_x * trial_x + trial_z * trial_z)
    rate = jnp.zeros_like(trial_norm)
    for _ in range(NEWTON):
        arg = scale_c * rate
        residual = trial_norm - ETA * rate - sigma_a * inverse_sinh(arg)
        slope = -ETA - sigma_a * scale_c / jnp.sqrt(1.0 + arg * arg)
        rate = rate - residual / slope
    return trial_norm, rate


def final_kernel(
    f_in, vel, xe, xo, ze, zo, ain, props, slots,
    v_out, rate_out, theta_out,
    pr, sj, sb, xs, ys, jp,
):
    grp = lax.axis_index("grp")
    blk = lax.axis_index("blk")
    lane, sub, jl, k, i_el = tile_iota()
    zero = jnp.zeros((8, 128), F32)
    lane_big = lax.broadcasted_iota(jnp.int32, (128, 128), 1)

    for c in range(3):
        for n in range(125):
            pr[c, n] = f_in[c, n] + row(vel, c, n)
    x_even = blk % 2 == 0
    for c in range(3):
        for q in range(5):
            for r in range(5):
                m = c * 25 + q * 5 + r
                ev, od = xe[m], xo[m]
                lo, hi = node(0, q, r), node(4, q, r)
                pr[c, lo, 0:2] = pr[c, lo, 0:2] + jnp.where(x_even, od, ev)
                pr[c, hi, 6:8] = pr[c, hi, 6:8] + jnp.where(x_even, ev, od)
    z_even = grp % 2 == 0
    zlo = [jnp.where(z_even, zo[g], ze[g]) for g in range(3)]
    zhi = [jnp.where(z_even, ze[g], zo[g]) for g in range(3)]

    xs[...] = jnp.zeros((128, 128), F32)
    slot4 = lax.broadcasted_iota(jnp.int32, (4, 128), 1) % 8
    for dg in (-1, 1):
        value = None
        for db in (-1, 1):
            ok = (grp + dg >= 0) & (grp + dg < N_GRP) & (blk + db >= 0) & (blk + db < N_BLK)
            at = jnp.where(ok, 8 * ((grp + dg) * N_BLK + blk + db), 0)
            part = ain[pl.ds(pl.multiple_of(at, 8), 4), :]
            part = jnp.where((slot4 >= 6) & ok, part, 0.0)
            value = roll(part, -6, 1) if value is None else value + part
        xs[pl.ds(31 if dg > 0 else 0, 4, stride=32), :] = value
    edges = xs[...].T
    for c in range(3):
        for p in range(5):
            for q in range(5):
                m = c * 25 + p * 5 + q
                n0, n4 = node(p, q, 0), node(p, q, 4)
                add0 = roll(zlo[m // 32], -(m % 32), 1)
                add4 = roll(zhi[m // 32], 31 - m % 32, 1)
                if p in (0, 4):
                    edge = edges[q * 24 + c * 8 : q * 24 + c * 8 + 8]
                    edge = jnp.where((sub < 4) == (p == 0), edge, 0.0)
                    add0, add4 = add0 + edge, add4 + edge
                pr[c, n0] = pr[c, n0] + jnp.where(k == 0, add0, 0.0)
                pr[c, n4] = pr[c, n4] + jnp.where(k == 31, add4, 0.0)

    for c in range(3):
        for p in range(5):
            for r in range(5):
                sj[pl.ds(8 * (c * 32 + p * 5 + r), 8), :] = fault_jump(
                    lambda q: pr[c, node(p, q, r)]
                )
    lane96 = lax.broadcasted_iota(jnp.int32, (96, 128), 1) // 32
    jump = None
    for i in range(4):
        part = roll(sj[pl.ds(2 * i + 1, 96, stride=8), :], 32 * i, 1)
        jump = part if jump is None else jnp.where(lane96 == i, part, jump)
    for i in range(4):
        ys[pl.ds(32 * i, 32), :] = ain[pl.ds(blk // 8 * 256 + 4 + i, 32, stride=8), :]
    par = ys[...].T
    t0x, t0z, scale_c, sigma_a = par[0:32], par[32:64], par[64:96], par[96:128]
    trial_x = t0x + ETA * jump[0:32]
    trial_z = t0z + ETA * jump[64:96]
    trial_norm, rate = solve(trial_x, trial_z, scale_c, sigma_a)
    keep = 1.0 - ETA * rate / jnp.maximum(trial_norm, TRACTION_FLOOR)
    push = (
        CORRECTION * (trial_x * keep - t0x),
        CORRECTION * ETA * jump[32:64],
        CORRECTION * (trial_z * keep - t0z),
    )
    for c in range(3):
        for i in range(4):
            sb[pl.ds(c * 256 + 2 * i + 1, 32, stride=8), :] = roll(push[c], -32 * i, 1)
            sb[pl.ds(c * 256 + 2 * i, 32, stride=8), :] = roll(push[c], 96 - 32 * i, 1)
    plus_at = (sub % 2 == 1) & (lane < 32)
    minus_at = (sub % 2 == 0) & (lane >= 96)
    for c in range(3):
        for p in range(5):
            for r in range(5):
                n0, n4 = node(p, 0, r), node(p, 4, r)
                push_back = sb[pl.ds(8 * (c * 32 + p * 5 + r), 8), :]
                pr[c, n0] = pr[c, n0] - jnp.where(plus_at, push_back, 0.0)
                pr[c, n4] = pr[c, n4] + jnp.where(minus_at, push_back, 0.0)
    for c in range(3):
        for n in range(125):
            v_out[c, n, :] = pr[c, n].reshape(1024)

    for u in range(4):
        for i in range(4):
            ys[pl.ds(8 * (u * 4 + i), 8), :] = ain[
                pl.ds(u * 256 + grp * 64 + i, 8, stride=8), :
            ]
    xs[...] = jnp.zeros((128, 128), F32)
    for u in range(4):
        for step, there, at, into in ((-1, grp > 0, 3, 0), (8, grp < N_GRP - 1, 0, 31)):
            source = jnp.where(there, (u * 32 + grp * 8 + step) * 8 + at, 0)
            value = ain[pl.ds(source, 1), :]
            xs[pl.ds(u * 32 + into, 1), :] = jnp.where(there, value, 0.0)
    body, ends = ys[...].T, xs[...].T
    first = jnp.where(grp_is(blk, 0), 1.0, 0.0).astype(F32)
    last = jnp.where(grp_is(blk, N_BLK - 1), 1.0, 0.0).astype(F32)

    def along_z(mat, p, c):
        at = p * 24 + c * 8
        t = mat[at : at + 8]
        low = jnp.where((sub == 0) & (lane >= 32), roll(roll(t, 32, 1), -5, 0), 0.0)
        high = jnp.where((sub == 4) & (lane < 96), roll(roll(t, -32, 1), -1, 0), 0.0)
        return t + low * first + high * last

    i_at, s_at = lane // 8 % 4, lane % 8
    for c in (0, 2):
        t = [along_z(body, p, c) for p in range(5)]
        end0, end4 = along_z(ends, 0, c), along_z(ends, 4, c)
        left = jnp.where(s_at == 0, end4, roll(t[4], -23, 1))
        right = jnp.where(s_at == 7, end0, roll(t[0], 23, 1))
        t[0], t[4] = (
            t[0] + jnp.where(i_at == 0, left, 0.0),
            t[4] + jnp.where(i_at == 3, right, 0.0),
        )
        for p in range(5):
            jp[c // 2, 5 * p : 5 * p + 5, :] = t[p][0:5]
    hot = slot_hot(slots[...])
    slot_jump = [
        lax.dot_general(
            jp[c], hot, (((1,), (0,)), ((), ())), precision=HIGHEST, preferred_element_type=F32
        )[0:25]
        for c in range(2)
    ]
    theta, a, b, length = props[0], props[1], props[2], props[3]
    scale_c = 0.5 * jnp.exp((FRICTION_REF + b * jnp.log(theta / length)) / a)
    _, rate = solve(
        props[4] + ETA * slot_jump[0], props[5] + ETA * slot_jump[1], scale_c, props[6] * a
    )
    rate_out[...] = rate
    theta_out[...] = theta + DT * (1.0 - rate * theta / length)


def grp_is(index, value):
    return index == value


def on_device(displacement, velocity, lame, fault_props, fault_slots):
    slots = fault_slots.reshape(1, 128)
    shape = lambda *s: jax.ShapeDtypeStruct(s, F32)
    vmem = lambda *s: pltpu.VMEM(s, F32)
    f, xe, xo, ze, zo, abuf = pl.pallas_call(
        force_kernel,
        name="force",
        out_shape=(
            shape(3, 125, 8, 128), shape(75, 2, 128), shape(75, 2, 128),
            shape(3, 8, 128), shape(3, 8, 128), shape(1024, 128),
        ),
        scratch_shapes=[
            vmem(3, 125, 8, 128), vmem(3, 125, 8, 128), vmem(1024, 128), vmem(128, 128),
            vmem(128, 128),
        ],
    )(displacement, velocity, lame, fault_props, slots)
    ain = lax.all_to_all(abuf, ("grp", "blk"), 0, 0, tiled=True)
    even_b = [(i, i ^ 1) for i in range(N_BLK)]
    odd_b = [(i, ((i + 1) ^ 1) - 1) for i in range(1, N_BLK - 1)]
    even_g = [(i, i ^ 1) for i in range(N_GRP)]
    odd_g = [(i, ((i + 1) ^ 1) - 1) for i in range(1, N_GRP - 1)]
    xe = lax.ppermute(xe, "blk", even_b)
    xo = lax.ppermute(xo, "blk", odd_b)
    ze = lax.ppermute(ze, "grp", even_g)
    zo = lax.ppermute(zo, "grp", odd_g)
    return pl.pallas_call(
        final_kernel,
        name="final",
        out_shape=(shape(3, 125, 1024), shape(25, 128), shape(25, 128)),
        scratch_shapes=[
            vmem(3, 125, 8, 128), vmem(768, 128), vmem(768, 128), vmem(128, 128),
            vmem(128, 128), vmem(2, 32, 128),
        ],
    )(f, velocity, xe, xo, ze, zo, ain, fault_props, slots)


def solution(mesh):
    both = ("grp", "blk")
    return jax.shard_map(
        on_device,
        mesh=mesh,
        in_specs=(P(None, None, both), P(None, None, both), P(None, both), P(None, None, both), P(both)),
        out_specs=(P(None, None, both), P(None, both), P(None, both)),
        check_vma=False,
    )
```

profile of v0, /device:TPU:1, one launch (start us, length us, event | category | flops | bytes accessed | tf_op | source)
XLA Modules:
  0.0 48.3 jit_solution(6260151166717991825)
XLA Ops:
  0.6 1.5 %copy.8.props = f32[7,25,128]{2,1,0:T(8,128)} copy(f32[7,25,128]{2,0,1:T(8,128)} %param.8) | data formatting | bytes 179200 | tf_op args[3]
  2.2 14.9 %force.1 = (f32[3,125,8,128]{3,2,1,0:T(8,128)}, f32[75,2,128]{2,1,0:T(2,128)}, f32[75,2,128]{2,1,0:T(2,128)}, f32[3,8,128]{2,1,0:T(8,128)}, f32[3,8,128]{2,1,0:T(8,128)}, /*index=5*/f32[1024,128]{1,0:T(8,128)}) custom-call(f32[3,125,1024]{2,1,0:T(8,128)} %disp.1, f32[3,125,1024]{2,1,0:T(8,128)} %vel.3, f32[2,1024]{1,0:T(2,128)} %lame.1, ...), custom_call_target="tpu_custom_call" | custom-call | tf_op jit(solution)/shard_map/force/pallas_call | solution.py:457
  17.1 11.5 %all-to-all-start = ((f32[128,8,128]{2,1,0:T(8,128)}), f32[128,8,128]{2,1,0:T(8,128)S(1)}, u32[]{:S(2)}, u32[]{:S(2)}) async-start(f32[128,8,128]{2,1,0:T(8,128)} %bitcast.4), calls=%async_computation | async-start | bytes 1048576 | tf_op jit(solution)/shard_map/all_to_all | solution.py:469
  28.6 1.1 %collective-permute-start = (f32[75,2,128]{2,1,0:T(2,128)}, f32[75,2,128]{2,1,0:T(2,128)S(1)}, u32[]{:S(2)}, u32[]{:S(2)}) collective-permute-start(f32[75,2,128]{2,1,0:T(2,128)} %get-tuple-element.10), channel_id=1, source_target_pairs={{0,1},{1,0},{2,3},{3,2},{4,5},{5,4},{6,7},{7,6},{8,9},{9,8},{10,11... | collective-permute-start | bytes 230408 | tf_op jit(solution)/shard_map/ppermute | solution.py:474
  29.8 2.6 %collective-permute-start.1 = (f32[75,2,128]{2,1,0:T(2,128)}, f32[75,2,128]{2,1,0:T(2,128)S(1)}, u32[]{:S(2)}, u32[]{:S(2)}) collective-permute-start(f32[75,2,128]{2,1,0:T(2,128)} %get-tuple-element.11), channel_id=1, source_target_pairs={{1,2},{2,1},{3,4},{4,3},{5,6},{6,5},{7,8},{8,7},{9,10},{10,9},{11,... | collective-permute-start | bytes 230408 | tf_op jit(solution)/shard_map/ppermute | solution.py:475
  32.3 1.3 %collective-permute-start.2 = (f32[3,8,128]{2,1,0:T(8,128)}, f32[3,8,128]{2,1,0:T(8,128)S(1)}, u32[]{:S(2)}, u32[]{:S(2)}) collective-permute-start(f32[3,8,128]{2,1,0:T(8,128)} %get-tuple-element.12), channel_id=1, source_target_pairs={{0,32},{32,0},{64,96},{96,64},{1,33},{33,1},{65,97},{97,65},{2,34}... | collective-permute-start | bytes 36872 | tf_op jit(solution)/shard_map/ppermute | solution.py:476
  33.6 0.7 %collective-permute-start.3 = (f32[3,8,128]{2,1,0:T(8,128)}, f32[3,8,128]{2,1,0:T(8,128)S(1)}, u32[]{:S(2)}, u32[]{:S(2)}) collective-permute-start(f32[3,8,128]{2,1,0:T(8,128)} %get-tuple-element.13), channel_id=1, source_target_pairs={{32,64},{64,32},{33,65},{65,33},{34,66},{66,34},{35,67},{67,35},{3... | collective-permute-start | bytes 36872 | tf_op jit(solution)/shard_map/ppermute | solution.py:477
  34.3 1.5 %collective-permute-done.2.ze = f32[3,8,128]{2,1,0:T(8,128)S(1)} collective-permute-done((f32[3,8,128]{2,1,0:T(8,128)}, f32[3,8,128]{2,1,0:T(8,128)S(1)}, u32[]{:S(2)}, u32[]{:S(2)}) %collective-permute-start.2) | collective-permute-done | bytes 12320 | tf_op jit(solution)/shard_map/ppermute | solution.py:476
  35.8 0.0 copy-start.3
  35.8 0.0 collective-permute-done.3.zo
  35.8 0.0 copy-start.4
  35.8 0.0 collective-permute-done.xe
  35.8 0.0 copy-start.1
  35.8 1.2 %collective-permute-done.1.xo = f32[75,2,128]{2,1,0:T(2,128)S(1)} collective-permute-done((f32[75,2,128]{2,1,0:T(2,128)}, f32[75,2,128]{2,1,0:T(2,128)S(1)}, u32[]{:S(2)}, u32[]{:S(2)}) %collective-permute-start.1) | collective-permute-done | bytes 76832 | tf_op jit(solution)/shard_map/ppermute | solution.py:475
  37.0 0.0 copy-start.2
  37.0 4.9 %all-to-all-done = f32[128,8,128]{2,1,0:T(8,128)S(1)} async-done(((f32[128,8,128]{2,1,0:T(8,128)}), f32[128,8,128]{2,1,0:T(8,128)S(1)}, u32[]{:S(2)}, u32[]{:S(2)}) %all-to-all-start) | async-done | bytes 524320 | tf_op jit(solution)/shard_map/all_to_all | solution.py:469
  41.9 0.0 copy-start
  41.9 0.0 copy-done.3
  41.9 0.0 copy-done.4
  41.9 0.0 copy-done.1
  41.9 0.0 copy-done.2
  41.9 0.8 %copy-done = f32[128,8,128]{2,1,0:T(8,128)} copy-done((f32[128,8,128]{2,1,0:T(8,128)}, f32[128,8,128]{2,1,0:T(8,128)S(1)}, u32[]{:S(2)}) %copy-start) | copy-done | bytes 524312
  42.7 5.6 %final.1 = (f32[3,125,1024]{2,1,0:T(8,128)}, f32[25,128]{1,0:T(8,128)}, f32[25,128]{1,0:T(8,128)}) custom-call(f32[3,125,8,128]{3,2,1,0:T(8,128)} %get-tuple-element.9.f_in, f32[3,125,1024]{2,1,0:T(8,128)} %vel.3, f32[75,2,128]{2,1,0:T(2,128)} %copy-done.1, f32[75,2,128]{2,1,0:T(2,128)} %copy-done.2, f32[3,8,128]{2,1,0:T(8,128)} %copy-done.3, ...), custom_call_target="tpu_custom_call" | custom-call | tf_op jit(solution)/shard_map/final/pallas_call | solution.py:478
Async XLA Ops:
  17.1 24.8 %all-to-all-start = ((f32[128,8,128]{2,1,0:T(8,128)}), f32[128,8,128]{2,1,0:T(8,128)S(1)}, u32[]{:S(2)}, u32[]{:S(2)}) async-start(f32[128,8,128]{2,1,0:T(8,128)} %bitcast.4), calls=%async_computation | async-start | bytes 1048576 | tf_op jit(solution)/shard_map/all_to_all | solution.py:469
  28.6 7.2 %collective-permute-start = (f32[75,2,128]{2,1,0:T(2,128)}, f32[75,2,128]{2,1,0:T(2,128)S(1)}, u32[]{:S(2)}, u32[]{:S(2)}) collective-permute-start(f32[75,2,128]{2,1,0:T(2,128)} %get-tuple-element.10), channel_id=1, source_target_pairs={{0,1},{1,0},{2,3},{3,2},{4,5},{5,4},{6,7},{7,6},{8,9},{9,8},{10,11... | collective-permute-start | bytes 230408 | tf_op jit(solution)/shard_map/ppermute | solution.py:474
  29.8 7.2 %collective-permute-start.1 = (f32[75,2,128]{2,1,0:T(2,128)}, f32[75,2,128]{2,1,0:T(2,128)S(1)}, u32[]{:S(2)}, u32[]{:S(2)}) collective-permute-start(f32[75,2,128]{2,1,0:T(2,128)} %get-tuple-element.11), channel_id=1, source_target_pairs={{1,2},{2,1},{3,4},{4,3},{5,6},{6,5},{7,8},{8,7},{9,10},{10,9},{11,... | collective-permute-start | bytes 230408 | tf_op jit(solution)/shard_map/ppermute | solution.py:475
  32.3 3.5 %collective-permute-start.2 = (f32[3,8,128]{2,1,0:T(8,128)}, f32[3,8,128]{2,1,0:T(8,128)S(1)}, u32[]{:S(2)}, u32[]{:S(2)}) collective-permute-start(f32[3,8,128]{2,1,0:T(8,128)} %get-tuple-element.12), channel_id=1, source_target_pairs={{0,32},{32,0},{64,96},{96,64},{1,33},{33,1},{65,97},{97,65},{2,34}... | collective-permute-start | bytes 36872 | tf_op jit(solution)/shard_map/ppermute | solution.py:476
  33.6 2.2 %collective-permute-start.3 = (f32[3,8,128]{2,1,0:T(8,128)}, f32[3,8,128]{2,1,0:T(8,128)S(1)}, u32[]{:S(2)}, u32[]{:S(2)}) collective-permute-start(f32[3,8,128]{2,1,0:T(8,128)} %get-tuple-element.13), channel_id=1, source_target_pairs={{32,64},{64,32},{33,65},{65,33},{34,66},{66,34},{35,67},{67,35},{3... | collective-permute-start | bytes 36872 | tf_op jit(solution)/shard_map/ppermute | solution.py:477
  35.8 6.1 %copy-start.3 = (f32[3,8,128]{2,1,0:T(8,128)}, f32[3,8,128]{2,1,0:T(8,128)S(1)}, u32[]{:S(2)}) copy-start(f32[3,8,128]{2,1,0:T(8,128)S(1)} %collective-permute-done.2.ze) | copy-start | bytes 36868
  35.8 6.1 %copy-start.4 = (f32[3,8,128]{2,1,0:T(8,128)}, f32[3,8,128]{2,1,0:T(8,128)S(1)}, u32[]{:S(2)}) copy-start(f32[3,8,128]{2,1,0:T(8,128)S(1)} %collective-permute-done.3.zo) | copy-start | bytes 36868
  35.8 6.1 %copy-start.1 = (f32[75,2,128]{2,1,0:T(2,128)}, f32[75,2,128]{2,1,0:T(2,128)S(1)}, u32[]{:S(2)}) copy-start(f32[75,2,128]{2,1,0:T(2,128)S(1)} %collective-permute-done.xe) | copy-start | bytes 230404
  37.0 5.0 %copy-start.2 = (f32[75,2,128]{2,1,0:T(2,128)}, f32[75,2,128]{2,1,0:T(2,128)S(1)}, u32[]{:S(2)}) copy-start(f32[75,2,128]{2,1,0:T(2,128)S(1)} %collective-permute-done.1.xo) | copy-start | bytes 230404
  41.9 0.8 %copy-start = (f32[128,8,128]{2,1,0:T(8,128)}, f32[128,8,128]{2,1,0:T(8,128)S(1)}, u32[]{:S(2)}) copy-start(f32[128,8,128]{2,1,0:T(8,128)S(1)} %all-to-all-done) | copy-start | bytes 1572868
where the time goes:
time: 49 us; the launch traced here: 48.3 us
  Pallas kernels  20.5 us (42%)
  starting transfers between devices  17.1 us (35%)
  waiting for transfers between devices  7.64 us (16%)
  local copies, waits for them, and re-layouts  2.35 us (5%)
  between operations  0.68 us (1%)
    pallas_call x1, Pallas kernels, on_device(): pl.pallas_call(force_kernel, name='force', out_shape=(shape(3, 125, 8, 12...  14.9 us
    all_to_all x1, starting transfers between devices, on_device(): ain = lax.all_to_all(abuf, ('grp', 'blk'), 0, 0, tiled=True)  11.5 us
    pallas_call x1, Pallas kernels, on_device(): pl.pallas_call(final_kernel, name='final', out_shape=(shape(3, 125, 1024)...  5.61 us
    all_to_all x1, waiting for transfers between devices, on_device(): ain = lax.all_to_all(abuf, ('grp', 'blk'), 0, 0, tiled=True)  4.94 us
    ppermute x1, starting transfers between devices, on_device(): xo = lax.ppermute(xo, 'blk', odd_b)  2.58 us
    unnamed x11, local copies, waits for them, and re-layouts  2.35 us
    ppermute x1, waiting for transfers between devices, on_device(): ze = lax.ppermute(ze, 'grp', even_g)  1.53 us
    ppermute x1, starting transfers between devices, on_device(): ze = lax.ppermute(ze, 'grp', even_g)  1.27 us
  transfers between devices with their start and end apart: 5, of which 3 were waited for; matrix products, arithmetic and copies ran while one was open for 0% of the time, Pallas kernels for 0%

commit v1 on v0

--- a/solution.py
+++ b/solution.py
@@ -91,8 +91,14 @@
     return (jnp.broadcast_to(slots, (128, 128)) == face).astype(F32)
 
 
-def fault_jump(get):
-    return get(0) - roll(roll(get(4), 32, 1), 1, 0)
+def fault_lanes(ref, rows):
+    block = lax.broadcasted_iota(jnp.int32, (rows, 128), 1) // 32
+    plus = [roll(ref[pl.ds(2 * i + 1, rows, stride=8), :], 32 * i, 1) for i in range(4)]
+    minus = [roll(ref[pl.ds(2 * i, rows, stride=8), :], 32 * i - 96, 1) for i in range(4)]
+    out = plus[0] - minus[0]
+    for i in range(1, 4):
+        out = jnp.where(block == i, plus[i] - minus[i], out)
+    return out
 
 
 def force_kernel(
@@ -148,54 +154,60 @@
 
     y4_in, y0_in = jl < 3, jl > 0
     x4_in, x0_in = i_el < 3, i_el > 0
-    for c in range(3):
-        for r in range(5):
-            f = [[f_out[c, node(p, q, r)] for q in range(5)] for p in range(5)]
-            for p in range(5):
-                if c == 0:
-                    s = [gx[1, node(p, q, r)] for q in range(5)]
-                else:
-                    s = [gy[c, node(p, q, r)] for q in range(5)]
-                out = line(M_TABLE, s)
-                for q in range(5):
-                    f[p][q] = f[p][q] + out[q]
-            for q in range(5):
-                out = line(M_TABLE, [gx[c, node(p, q, r)] for p in range(5)])
-                for p in range(5):
-                    f[p][q] = f[p][q] + out[p]
-            for p in range(5):
-                avg = 0.5 * (f[p][4] + roll(f[p][0], -32, 1))
-                f[p][0] = jnp.where(y0_in, roll(avg, 32, 1), f[p][0])
-                f[p][4] = jnp.where(y4_in, avg, f[p][4])
-            for q in range(5):
-                avg = 0.5 * (f[4][q] + roll(f[0][q], -2, 0))
-                f[0][q] = jnp.where(x0_in, roll(avg, 2, 0), f[0][q] * x0)
-                f[4][q] = jnp.where(x4_in, avg, f[4][q] * x4)
-            for p in range(5):
-                for q in range(5):
-                    f_out[c, node(p, q, r)] = f[p][q]
-
     z4_in, z0_in = k < 31, k > 0
     zero = jnp.zeros((8, 128), F32)
-    zlo, zhi = [zero] * 3, [zero] * 3
-    for c in range(3):
+
+    def xy_parts(c, r):
+        f = [[f_out[c, node(p, q, r)] for q in range(5)] for p in range(5)]
+        for p in range(5):
+            if c == 0:
+                s = [gx[1, node(p, q, r)] for q in range(5)]
+            else:
+                s = [gy[c, node(p, q, r)] for q in range(5)]
+            out = line(M_TABLE, s)
+            for q in range(5):
+                f[p][q] = f[p][q] + out[q]
+        for q in range(5):
+            out = line(M_TABLE, [gx[c, node(p, q, r)] for p in range(5)])
+            for p in range(5):
+                f[p][q] = f[p][q] + out[p]
+        for p in range(5):
+            up, down = roll(f[p][0], -32, 1), roll(f[p][4], 32, 1)
+            f[p][0], f[p][4] = (
+                jnp.where(y0_in, 0.5 * (f[p][0] + down), f[p][0]),
+                jnp.where(y4_in, 0.5 * (f[p][4] + up), f[p][4]),
+            )
+        for q in range(5):
+            avg = 0.5 * (f[4][q] + roll(f[0][q], -2, 0))
+            f[0][q] = jnp.where(x0_in, roll(avg, 2, 0), f[0][q] * x0)
+            f[4][q] = jnp.where(x4_in, avg, f[4][q] * x4)
+        for p in range(5):
+            for q in range(5):
+                f_out[c, node(p, q, r)] = f[p][q]
+
+    for c in range(3):
+        xy_parts(c, 0)
+        xy_parts(c, 4)
         for p in range(5):
             for q in range(5):
                 n0, n4 = node(p, q, 0), node(p, q, 4)
                 a0, a4 = f_out[c, n0], f_out[c, n4]
-                avg = 0.5 * (a4 + roll(a0, -1, 1))
-                a0 = jnp.where(z0_in, roll(avg, 1, 1), a0 * z0)
-                a4 = jnp.where(z4_in, avg, a4 * z4)
-                f_out[c, n0] = a0
-                f_out[c, n4] = a4
-                m = c * 25 + p * 5 + q
-                at = k == m % 32
-                zlo[m // 32] = jnp.where(at, roll(a0, m % 32, 1), zlo[m // 32])
-                zhi[m // 32] = jnp.where(at, roll(a4, m % 32 - 31, 1), zhi[m // 32])
+                up, down = roll(a0, -1, 1), roll(a4, 1, 1)
+                f_out[c, n0] = jnp.where(z0_in, 0.5 * (a0 + down), a0 * z0)
+                f_out[c, n4] = jnp.where(z4_in, 0.5 * (a4 + up), a4 * z4)
+        for r in (1, 2, 3):
+            xy_parts(c, r)
+
     z_even = grp % 2 == 0
     for g in range(3):
-        ze_out[g] = jnp.where(z_even, zhi[g], zlo[g])
-        zo_out[g] = jnp.where(z_even, zlo[g], zhi[g])
+        zlo, zhi = zero, zero
+        for m in range(32 * g, min(75, 32 * g + 32)):
+            c, pq = m // 25, m % 25
+            at = k == m % 32
+            zlo = jnp.where(at, roll(f_out[c, 5 * pq], m % 32, 1), zlo)
+            zhi = jnp.where(at, roll(f_out[c, 5 * pq + 4], m % 32 - 31, 1), zhi)
+        ze_out[g] = jnp.where(z_even, zhi, zlo)
+        zo_out[g] = jnp.where(z_even, zlo, zhi)
 
     x_even = blk % 2 == 0
     for c in range(3):
@@ -211,34 +223,28 @@
         abuf[pl.ds(8 * t, 8), :] = zero
     own_x = {0: jnp.where(x0_in, 1.0, x0), 4: jnp.where(x4_in, 1.0, x4)}
     own_z = {0: jnp.where(z0_in, 1.0, z0), 4: jnp.where(z4_in, 1.0, z4)}
+    odd_sub = sub % 2 == 1
     for p in range(5):
-        for c in range(3):
-            jump = [None] * 5
+        for cc in range(2):
+            c = 2 * cc
+            sides = [None] * 5
             for r in range(5):
                 own = None
                 for part in (own_x.get(p), own_z.get(r)):
                     if part is not None:
                         own = part if own is None else own * part
-
-                def side(q, own=own, r=r):
-                    v = row(vel, c, node(p, q, r))
-                    return f_out[c, node(p, q, r)] + (v if own is None else v * own)
-
-                jump[r] = fault_jump(side)
-                sj[pl.ds(8 * (p * 24 + c * 8 + r), 8), :] = jump[r]
-            extra = jnp.where(k == 0, roll(jump[4], -31, 1), 0.0)
-            extra = jnp.where(k == 31, roll(jump[0], 31, 1), extra)
-            sj[pl.ds(8 * (p * 24 + c * 8 + 5), 8), :] = extra
-            sj[pl.ds(8 * (p * 24 + c * 8 + 6), 8), :] = zero
-            sj[pl.ds(8 * (p * 24 + c * 8 + 7), 8), :] = zero
-    for t in range(120, 128):
-        sj[pl.ds(8 * t, 8), :] = zero
-    lane_big = lax.broadcasted_iota(jnp.int32, (128, 128), 1)
-    y = None
-    for i in range(4):
-        part = roll(sj[pl.ds(2 * i + 1, 128, stride=8), :], 32 * i, 1)
-        y = part if y is None else jnp.where(lane_big // 32 == i, part, y)
-    yt = y.T
+                n0, n4 = node(p, 0, r), node(p, 4, r)
+                v = jnp.where(odd_sub, row(vel, c, n0), row(vel, c, n4))
+                f = jnp.where(odd_sub, f_out[c, n0], f_out[c, n4])
+                sides[r] = f + (v if own is None else v * own)
+                sj[pl.ds(8 * (p * 16 + cc * 8 + r), 8), :] = sides[r]
+            extra = jnp.where(k == 0, roll(sides[4], -31, 1), 0.0)
+            extra = jnp.where(k == 31, roll(sides[0], 31, 1), extra)
+            sj[pl.ds(8 * (p * 16 + cc * 8 + 5), 8), :] = extra
+            sj[pl.ds(8 * (p * 16 + cc * 8 + 6), 8), :] = zero
+            sj[pl.ds(8 * (p * 16 + cc * 8 + 7), 8), :] = zero
+    y = fault_lanes(sj, 80)
+    yt = jnp.concatenate([y, jnp.zeros((48, 128), F32)]).T
     dest = blk // 8
 
     def put_jump(d):
@@ -256,11 +262,11 @@
         put_jump(dest - 1)
 
     xs[...] = jnp.zeros((128, 128), F32)
-    theta, a, b, length = props[0], props[1], props[2], props[3]
-    xs[0:25] = props[4]
-    xs[32:57] = props[5]
+    theta, a, b, length, pre_x, pre_z, sigma = (props[:, i, :] for i in range(7))
+    xs[0:25] = pre_x
+    xs[32:57] = pre_z
     xs[64:89] = 0.5 * jnp.exp((FRICTION_REF + b * jnp.log(theta / length)) / a)
-    xs[96:121] = props[6] * a
+    xs[96:121] = sigma * a
     packed = lax.dot_general(
         slot_hot(slots[...]), xs[...], (((1,), (1,)), ((), ())),
         precision=HIGHEST, preferred_element_type=F32,
@@ -355,17 +361,14 @@
                 pr[c, n0] = pr[c, n0] + jnp.where(k == 0, add0, 0.0)
                 pr[c, n4] = pr[c, n4] + jnp.where(k == 31, add4, 0.0)
 
+    odd_sub = sub % 2 == 1
     for c in range(3):
         for p in range(5):
             for r in range(5):
-                sj[pl.ds(8 * (c * 32 + p * 5 + r), 8), :] = fault_jump(
-                    lambda q: pr[c, node(p, q, r)]
+                sj[pl.ds(8 * (c * 32 + p * 5 + r), 8), :] = jnp.where(
+                    odd_sub, pr[c, node(p, 0, r)], pr[c, node(p, 4, r)]
                 )
-    lane96 = lax.broadcasted_iota(jnp.int32, (96, 128), 1) // 32
-    jump = None
-    for i in range(4):
-        part = roll(sj[pl.ds(2 * i + 1, 96, stride=8), :], 32 * i, 1)
-        jump = part if jump is None else jnp.where(lane96 == i, part, jump)
+    jump = fault_lanes(sj, 96)
     for i in range(4):
         ys[pl.ds(32 * i, 32), :] = ain[pl.ds(blk // 8 * 256 + 4 + i, 32, stride=8), :]
     par = ys[...].T
@@ -412,7 +415,7 @@
     last = jnp.where(grp_is(blk, N_BLK - 1), 1.0, 0.0).astype(F32)
 
     def along_z(mat, p, c):
-        at = p * 24 + c * 8
+        at = p * 16 + c * 4
         t = mat[at : at + 8]
         low = jnp.where((sub == 0) & (lane >= 32), roll(roll(t, 32, 1), -5, 0), 0.0)
         high = jnp.where((sub == 4) & (lane < 96), roll(roll(t, -32, 1), -1, 0), 0.0)
@@ -437,10 +440,10 @@
         )[0:25]
         for c in range(2)
     ]
-    theta, a, b, length = props[0], props[1], props[2], props[3]
+    theta, a, b, length, pre_x, pre_z, sigma = (props[:, i, :] for i in range(7))
     scale_c = 0.5 * jnp.exp((FRICTION_REF + b * jnp.log(theta / length)) / a)
     _, rate = solve(
-        props[4] + ETA * slot_jump[0], props[5] + ETA * slot_jump[1], scale_c, props[6] * a
+        pre_x + ETA * slot_jump[0], pre_z + ETA * slot_jump[1], scale_c, sigma * a
     )
     rate_out[...] = rate
     theta_out[...] = theta + DT * (1.0 - rate * theta / length)
@@ -450,11 +453,19 @@
     return index == value
 
 
-def on_device(displacement, velocity, lame, fault_props, fault_slots):
-    slots = fault_slots.reshape(1, 128)
-    shape = lambda *s: jax.ShapeDtypeStruct(s, F32)
-    vmem = lambda *s: pltpu.VMEM(s, F32)
-    f, xe, xo, ze, zo, abuf = pl.pallas_call(
+VMEM_LIMIT = 24 << 20
+
+
+def shape(*dims):
+    return jax.ShapeDtypeStruct(dims, F32)
+
+
+def vmem(*dims):
+    return pltpu.VMEM(dims, F32)
+
+
+def force_call(*args):
+    return pl.pallas_call(
         force_kernel,
         name="force",
         out_shape=(
@@ -462,10 +473,17 @@
             shape(3, 8, 128), shape(3, 8, 128), shape(1024, 128),
         ),
         scratch_shapes=[
-            vmem(3, 125, 8, 128), vmem(3, 125, 8, 128), vmem(1024, 128), vmem(128, 128),
+            vmem(3, 125, 8, 128), vmem(3, 125, 8, 128), vmem(640, 128), vmem(128, 128),
             vmem(128, 128),
         ],
-    )(displacement, velocity, lame, fault_props, slots)
+        compiler_params=pltpu.CompilerParams(vmem_limit_bytes=VMEM_LIMIT),
+    )(*args)
+
+
+def on_device(displacement, velocity, lame, fault_props, fault_slots):
+    slots = fault_slots.reshape(1, 128)
+    fault_props = jnp.transpose(fault_props, (1, 0, 2))
+    f, xe, xo, ze, zo, abuf = force_call(displacement, velocity, lame, fault_props, slots)
     ain = lax.all_to_all(abuf, ("grp", "blk"), 0, 0, tiled=True)
     even_b = [(i, i ^ 1) for i in range(N_BLK)]
     odd_b = [(i, ((i + 1) ^ 1) - 1) for i in range(1, N_BLK - 1)]
@@ -483,6 +501,7 @@
             vmem(3, 125, 8, 128), vmem(768, 128), vmem(768, 128), vmem(128, 128),
             vmem(128, 128), vmem(2, 32, 128),
         ],
+        compiler_params=pltpu.CompilerParams(vmem_limit_bytes=VMEM_LIMIT),
     )(f, velocity, xe, xo, ze, zo, ain, fault_props, slots)
 
 

time: 49 us -> 41.7 us (0.85)
  Pallas kernels: 20.5 us -> 7.83 us
  local copies, waits for them, and re-layouts: 2.35 us -> 7.58 us
    pallas_call x1, Pallas kernels: 14.9 us -> 4.23 us  [force_call(): pl.pallas_call(force_kernel, name='force', out_shape=(shape(3, 125, 8, 12...]
    unnamed x11 -> x20, local copies, waits for them, and re-layouts: 2.35 us -> 7.58 us
    pallas_call x1, Pallas kernels: 5.61 us -> 3.6 us  [on_device(): pl.pallas_call(final_kernel, name='final', out_shape=(shape(3, 125, 1024)...]
where the time goes in v1:
time: 41.7 us; the launch traced here: 40.9 us
  starting transfers between devices  17.1 us (41%)
  Pallas kernels  7.83 us (19%)
  waiting for transfers between devices  7.66 us (18%)
  local copies, waits for them, and re-layouts  7.58 us (18%)
  between operations  0.69 us (2%)
    all_to_all x1, starting transfers between devices, on_device(): ain = lax.all_to_all(abuf, ('grp', 'blk'), 0, 0, tiled=True)  11.5 us
    unnamed x20, local copies, waits for them, and re-layouts  7.58 us
    all_to_all x1, waiting for transfers between devices, on_device(): ain = lax.all_to_all(abuf, ('grp', 'blk'), 0, 0, tiled=True)  4.94 us
    pallas_call x1, Pallas kernels, force_call(): pl.pallas_call(force_kernel, name='force', out_shape=(shape(3, 125, 8, 12...  4.23 us
    pallas_call x1, Pallas kernels, on_device(): pl.pallas_call(final_kernel, name='final', out_shape=(shape(3, 125, 1024)...  3.6 us
    ppermute x1, starting transfers between devices, on_device(): xo = lax.ppermute(xo, 'blk', odd_b)  2.58 us
    ppermute x1, waiting for transfers between devices, on_device(): ze = lax.ppermute(ze, 'grp', even_g)  1.45 us
    ppermute x1, starting transfers between devices, on_device(): ze = lax.ppermute(ze, 'grp', even_g)  1.27 us
  transfers between devices with their start and end apart: 5, of which 3 were waited for; matrix products, arithmetic and copies ran while one was open for 0% of the time, Pallas kernels for 0%

profile of v1, /device:TPU:1, one launch (start us, length us, event | category | flops | bytes accessed | tf_op | source)
XLA Modules:
  0.0 40.9 jit_solution(8376286798279541289)
XLA Ops:
  0.6 0.0 copy-start
  0.6 1.4 %copy-done = f32[3,125,1024]{2,1,0:T(8,128)S(1)} copy-done((f32[3,125,1024]{2,1,0:T(8,128)S(1)}, f32[3,125,1024]{2,1,0:T(8,128)}, u32[]{:S(2)}) %copy-start) | copy-done | bytes 1536024
  2.0 1.4 %copy-done.2 = f32[3,125,1024]{2,1,0:T(8,128)S(1)} copy-done((f32[3,125,1024]{2,1,0:T(8,128)S(1)}, f32[3,125,1024]{2,1,0:T(8,128)}, u32[]{:S(2)}) %copy-start.2) | copy-done | bytes 1536024
  3.5 0.9 %copy-done.5 = f32[7,25,128]{2,0,1:T(8,128)S(1)} copy-done((f32[7,25,128]{2,0,1:T(8,128)S(1)}, f32[7,25,128]{2,0,1:T(8,128)}, u32[]{:S(2)}) %copy-start.5) | copy-done | bytes 89624
  4.3 0.7 %copy-done.7 = f32[2,1024]{1,0:T(2,128)S(1)} copy-done((f32[2,1024]{1,0:T(2,128)S(1)}, f32[2,1024]{1,0:T(2,128)}, u32[]{:S(2)}) %copy-start.7) | copy-done | bytes 8216
  5.0 0.7 %copy-done.8 = s32[128]{0:T(128)S(1)} copy-done((s32[128]{0:T(128)S(1)}, s32[128]{0:T(128)}, u32[]{:S(2)}) %copy-start.8) | copy-done | bytes 536
  5.7 4.2 %force.1 = (f32[3,125,8,128]{3,2,1,0:T(8,128)S(1)}, f32[75,2,128]{2,1,0:T(2,128)S(1)}, f32[75,2,128]{2,1,0:T(2,128)S(1)}, f32[3,8,128]{2,1,0:T(8,128)S(1)}, f32[...) custom-call(f32[3,125,1024]{2,1,0:T(8,128)S(1)} %copy-done.2, f32[3,125,1024]{2,1,0:T(8,128)S(1)} %copy-done, ...), custom_call_target="tpu_custom_call" | custom-call | tf_op jit(solution)/shard_map/force/pallas_call | solution.py:468
  9.9 1.1 %copy-done.3 = f32[3,125,8,128]{3,2,1,0:T(8,128)} copy-done((f32[3,125,8,128]{3,2,1,0:T(8,128)}, f32[3,125,8,128]{3,2,1,0:T(8,128)S(1)}, u32[]{:S(2)}) %copy-start.3) | copy-done | bytes 1536024
  11.1 11.5 %all-to-all-start = ((f32[128,8,128]{2,1,0:T(8,128)}), f32[128,8,128]{2,1,0:T(8,128)S(1)}, u32[]{:S(2)}, u32[]{:S(2)}) async-start(f32[128,8,128]{2,1,0:T(8,128)} %bitcast.2), calls=%async_computation | async-start | bytes 1048576 | tf_op jit(solution)/shard_map/all_to_all | solution.py:487
  22.6 1.1 %collective-permute-start = (f32[75,2,128]{2,1,0:T(2,128)S(1)}, f32[75,2,128]{2,1,0:T(2,128)S(1)}, u32[]{:S(2)}, u32[]{:S(2)}) collective-permute-start(f32[75,2,128]{2,1,0:T(2,128)S(1)} %get-tuple-element.10), channel_id=1, source_target_pairs={{0,1},{1,0},{2,3},{3,2},{4,5},{5,4},{6,7},{7,6},{8,9},{9,8},{10,11... | collective-permute-start | bytes 230408 | tf_op jit(solution)/shard_map/ppermute | solution.py:492
  23.7 2.6 %collective-permute-start.1 = (f32[75,2,128]{2,1,0:T(2,128)S(1)}, f32[75,2,128]{2,1,0:T(2,128)S(1)}, u32[]{:S(2)}, u32[]{:S(2)}) collective-permute-start(f32[75,2,128]{2,1,0:T(2,128)S(1)} %get-tuple-element.11), channel_id=1, source_target_pairs={{1,2},{2,1},{3,4},{4,3},{5,6},{6,5},{7,8},{8,7},{9,10},{10,9},{11,... | collective-permute-start | bytes 230408 | tf_op jit(solution)/shard_map/ppermute | solution.py:493
  26.3 1.3 %collective-permute-start.2 = (f32[3,8,128]{2,1,0:T(8,128)S(1)}, f32[3,8,128]{2,1,0:T(8,128)S(1)}, u32[]{:S(2)}, u32[]{:S(2)}) collective-permute-start(f32[3,8,128]{2,1,0:T(8,128)S(1)} %get-tuple-element.12), channel_id=1, source_target_pairs={{0,32},{32,0},{64,96},{96,64},{1,33},{33,1},{65,97},{97,65},{2,34}... | collective-permute-start | bytes 36872 | tf_op jit(solution)/shard_map/ppermute | solution.py:494
  27.6 0.7 %collective-permute-start.3 = (f32[3,8,128]{2,1,0:T(8,128)S(1)}, f32[3,8,128]{2,1,0:T(8,128)S(1)}, u32[]{:S(2)}, u32[]{:S(2)}) collective-permute-start(f32[3,8,128]{2,1,0:T(8,128)S(1)} %get-tuple-element.13), channel_id=1, source_target_pairs={{32,64},{64,32},{33,65},{65,33},{34,66},{66,34},{35,67},{67,35},{3... | collective-permute-start | bytes 36872 | tf_op jit(solution)/shard_map/ppermute | solution.py:495
  28.2 1.5 %collective-permute-done.2.ze = f32[3,8,128]{2,1,0:T(8,128)S(1)} collective-permute-done((f32[3,8,128]{2,1,0:T(8,128)S(1)}, f32[3,8,128]{2,1,0:T(8,128)S(1)}, u32[]{:S(2)}, u32[]{:S(2)}) %collective-permute-start.2) | collective-permute-done | bytes 12320 | tf_op jit(solution)/shard_map/ppermute | solution.py:494
  29.7 0.0 collective-permute-done.3.zo
  29.7 0.0 collective-permute-done.xe
  29.7 1.3 %collective-permute-done.1.xo = f32[75,2,128]{2,1,0:T(2,128)S(1)} collective-permute-done((f32[75,2,128]{2,1,0:T(2,128)S(1)}, f32[75,2,128]{2,1,0:T(2,128)S(1)}, u32[]{:S(2)}, u32[]{:S(2)}) %collective-permute-start.1) | collective-permute-done | bytes 76832 | tf_op jit(solution)/shard_map/ppermute | solution.py:493
  30.9 4.9 %all-to-all-done = f32[128,8,128]{2,1,0:T(8,128)S(1)} async-done(((f32[128,8,128]{2,1,0:T(8,128)}), f32[128,8,128]{2,1,0:T(8,128)S(1)}, u32[]{:S(2)}, u32[]{:S(2)}) %all-to-all-start) | async-done | bytes 524320 | tf_op jit(solution)/shard_map/all_to_all | solution.py:487
  35.9 0.0 copy-done.1
  35.9 0.0 copy-done.6
  35.9 0.0 copy-done.9
  35.9 0.0 copy-start.4
  35.9 1.4 %copy-done.4 = f32[3,125,8,128]{3,2,1,0:T(8,128)S(1)} copy-done((f32[3,125,8,128]{3,2,1,0:T(8,128)S(1)}, f32[3,125,8,128]{3,2,1,0:T(8,128)}, u32[]{:S(2)}) %copy-start.4) | copy-done | bytes 1536024
  37.3 3.6 %final.1 = (f32[3,125,1024]{2,1,0:T(8,128)}, f32[25,128]{1,0:T(8,128)}, f32[25,128]{1,0:T(8,128)}) custom-call(f32[3,125,8,128]{3,2,1,0:T(8,128)S(1)} %copy-done.4, f32[3,125,1024]{2,1,0:T(8,128)S(1)} %copy-done.1, f32[75,2,128]{2,1,0:T(2,128)S(1)} %collective-permute-done.xe, f32[75,2,128]{2,1,0:T(2,128)S(1)} %collective-permute-done.1.xo, ...), custom_call_target="tpu_custom_call" | custom-call | tf_op jit(solution)/shard_map/final/pallas_call | solution.py:496
  (8 shorter events, 0.0 us)
Async XLA Ops:
  0.6 1.4 %copy-start = (f32[3,125,1024]{2,1,0:T(8,128)S(1)}, f32[3,125,1024]{2,1,0:T(8,128)}, u32[]{:S(2)}) copy-start(f32[3,125,1024]{2,1,0:T(8,128)} %vel.3) | copy-start | bytes 4608004
  2.0 1.4 %copy-start.2 = (f32[3,125,1024]{2,1,0:T(8,128)S(1)}, f32[3,125,1024]{2,1,0:T(8,128)}, u32[]{:S(2)}) copy-start(f32[3,125,1024]{2,1,0:T(8,128)} %disp.1) | copy-start | bytes 4608004
  3.4 0.9 %copy-start.5 = (f32[7,25,128]{2,0,1:T(8,128)S(1)}, f32[7,25,128]{2,0,1:T(8,128)}, u32[]{:S(2)}) copy-start(f32[7,25,128]{2,0,1:T(8,128)} %param.8) | copy-start | bytes 268804
  4.3 0.7 %copy-start.7 = (f32[2,1024]{1,0:T(2,128)S(1)}, f32[2,1024]{1,0:T(2,128)}, u32[]{:S(2)}) copy-start(f32[2,1024]{1,0:T(2,128)} %lame.1) | copy-start | bytes 24580
  5.0 0.7 %copy-start.8 = (s32[128]{0:T(128)S(1)}, s32[128]{0:T(128)}, u32[]{:S(2)}) copy-start(s32[128]{0:T(128)} %param.9) | copy-start | bytes 1540
  5.7 30.2 %copy-start.1 = (f32[3,125,1024]{2,1,0:T(8,128)S(1)}, f32[3,125,1024]{2,1,0:T(8,128)}, u32[]{:S(2)}) copy-start(f32[3,125,1024]{2,1,0:T(8,128)} %vel.3) | copy-start | bytes 4608004
  5.7 30.2 %copy-start.6 = (f32[7,25,128]{2,0,1:T(8,128)S(1)}, f32[7,25,128]{2,0,1:T(8,128)}, u32[]{:S(2)}) copy-start(f32[7,25,128]{2,0,1:T(8,128)} %param.8) | copy-start | bytes 268804
  5.7 30.2 %copy-start.9 = (s32[128]{0:T(128)S(1)}, s32[128]{0:T(128)}, u32[]{:S(2)}) copy-start(s32[128]{0:T(128)} %param.9) | copy-start | bytes 1540
  9.9 1.1 %copy-start.3 = (f32[3,125,8,128]{3,2,1,0:T(8,128)}, f32[3,125,8,128]{3,2,1,0:T(8,128)S(1)}, u32[]{:S(2)}) copy-start(f32[3,125,8,128]{3,2,1,0:T(8,128)S(1)} %get-tuple-element.9.f_in) | copy-start | bytes 4608004
  11.1 24.8 %all-to-all-start = ((f32[128,8,128]{2,1,0:T(8,128)}), f32[128,8,128]{2,1,0:T(8,128)S(1)}, u32[]{:S(2)}, u32[]{:S(2)}) async-start(f32[128,8,128]{2,1,0:T(8,128)} %bitcast.2), calls=%async_computation | async-start | bytes 1048576 | tf_op jit(solution)/shard_map/all_to_all | solution.py:487
  22.6 7.1 %collective-permute-start = (f32[75,2,128]{2,1,0:T(2,128)S(1)}, f32[75,2,128]{2,1,0:T(2,128)S(1)}, u32[]{:S(2)}, u32[]{:S(2)}) collective-permute-start(f32[75,2,128]{2,1,0:T(2,128)S(1)} %get-tuple-element.10), channel_id=1, source_target_pairs={{0,1},{1,0},{2,3},{3,2},{4,5},{5,4},{6,7},{7,6},{8,9},{9,8},{10,11... | collective-permute-start | bytes 230408 | tf_op jit(solution)/shard_map/ppermute | solution.py:492
  23.7 7.2 %collective-permute-start.1 = (f32[75,2,128]{2,1,0:T(2,128)S(1)}, f32[75,2,128]{2,1,0:T(2,128)S(1)}, u32[]{:S(2)}, u32[]{:S(2)}) collective-permute-start(f32[75,2,128]{2,1,0:T(2,128)S(1)} %get-tuple-element.11), channel_id=1, source_target_pairs={{1,2},{2,1},{3,4},{4,3},{5,6},{6,5},{7,8},{8,7},{9,10},{10,9},{11,... | collective-permute-start | bytes 230408 | tf_op jit(solution)/shard_map/ppermute | solution.py:493
  26.3 3.4 %collective-permute-start.2 = (f32[3,8,128]{2,1,0:T(8,128)S(1)}, f32[3,8,128]{2,1,0:T(8,128)S(1)}, u32[]{:S(2)}, u32[]{:S(2)}) collective-permute-start(f32[3,8,128]{2,1,0:T(8,128)S(1)} %get-tuple-element.12), channel_id=1, source_target_pairs={{0,32},{32,0},{64,96},{96,64},{1,33},{33,1},{65,97},{97,65},{2,34}... | collective-permute-start | bytes 36872 | tf_op jit(solution)/shard_map/ppermute | solution.py:494
  27.6 2.1 %collective-permute-start.3 = (f32[3,8,128]{2,1,0:T(8,128)S(1)}, f32[3,8,128]{2,1,0:T(8,128)S(1)}, u32[]{:S(2)}, u32[]{:S(2)}) collective-permute-start(f32[3,8,128]{2,1,0:T(8,128)S(1)} %get-tuple-element.13), channel_id=1, source_target_pairs={{32,64},{64,32},{33,65},{65,33},{34,66},{66,34},{35,67},{67,35},{3... | collective-permute-start | bytes 36872 | tf_op jit(solution)/shard_map/ppermute | solution.py:495
  35.9 1.4 %copy-start.4 = (f32[3,125,8,128]{3,2,1,0:T(8,128)S(1)}, f32[3,125,8,128]{3,2,1,0:T(8,128)}, u32[]{:S(2)}) copy-start(f32[3,125,8,128]{3,2,1,0:T(8,128)} %copy-done.3) | copy-start | bytes 4608004

commit v2 on v1

v2 whole, which is shorter than its diff:
```python
import jax
import jax.numpy as jnp
import numpy as np
from jax import lax
from jax.experimental import pallas as pl
from jax.experimental.pallas import tpu as pltpu
from jax.sharding import PartitionSpec as P

NEWTON = 3
GLL_POINTS = np.array([-1.0, -np.sqrt(3.0 / 7.0), 0.0, np.sqrt(3.0 / 7.0), 1.0])
GLL_WEIGHTS = np.array([0.1, 49.0 / 90.0, 32.0 / 45.0, 49.0 / 90.0, 0.1])
DT = 0.01
W_END = 0.1
ETA = W_END / (2.0 * DT)
CORRECTION = DT / W_END
FRICTION_REF = 0.6
TRACTION_FLOOR = 1.0
N_GRP = 4
N_BLK = 32
F32 = jnp.float32
HIGHEST = lax.Precision.HIGHEST


def derivative_table():
    x = GLL_POINTS
    bary = [1.0 / np.prod([x[c] - x[o] for o in range(5) if o != c]) for c in range(5)]
    table = np.zeros((5, 5))
    for r in range(5):
        for c in range(5):
            if r != c:
                table[r, c] = bary[c] / bary[r] / (x[r] - x[c])
        table[r, r] = -np.sum(table[r])
    return table


D_TABLE = derivative_table()
M_TABLE = -DT * D_TABLE.T * GLL_WEIGHTS[None, :] / GLL_WEIGHTS[:, None]


def line(table, u):
    e0, e1 = u[0] + u[4], u[1] + u[3]
    o0, o1 = u[0] - u[4], u[1] - u[3]
    out = [None] * 5
    for i in range(2):
        even = (
            float((table[i, 0] + table[i, 4]) / 2) * e0
            + float((table[i, 1] + table[i, 3]) / 2) * e1
            + float(table[i, 2]) * u[2]
        )
        odd = (
            float((table[i, 0] - table[i, 4]) / 2) * o0
            + float((table[i, 1] - table[i, 3]) / 2) * o1
        )
        out[i] = odd + even
        out[4 - i] = odd - even
    out[2] = float(table[2, 0]) * o0 + float(table[2, 1]) * o1
    return out


def node(p, q, r):
    return 25 * p + 5 * q + r


def roll(x, shift, axis):
    shift = shift % x.shape[axis]
    return x if shift == 0 else pltpu.roll(x, shift, axis)


def row(ref, c, n):
    return ref[c, n, :].reshape(8, 128)


def tile_iota():
    lane = lax.broadcasted_iota(jnp.int32, (8, 128), 1)
    sub = lax.broadcasted_iota(jnp.int32, (8, 128), 0)
    return lane, sub, lane // 32, lane % 32, sub // 2


def inverse_sinh(value):
    return jnp.log(value + jnp.sqrt(1.0 + value * value))


def own_scales(grp, blk):
    half = lambda has: jnp.where(has, 0.5, 1.0).astype(F32)
    return half(blk > 0), half(blk < N_BLK - 1), half(grp > 0), half(grp < N_GRP - 1)


def slot_hot(slots):
    r = lax.broadcasted_iota(jnp.int32, (128, 128), 0)
    face = (r % 8) * 16 + (r // 8 % 4) * 4 + r // 32
    return (jnp.broadcast_to(slots, (128, 128)) == face).astype(F32)


def fault_lanes(ref, rows):
    block = lax.broadcasted_iota(jnp.int32, (rows, 128), 1) // 32
    plus = [roll(ref[pl.ds(2 * i + 1, rows, stride=8), :], 32 * i, 1) for i in range(4)]
    minus = [roll(ref[pl.ds(2 * i, rows, stride=8), :], 32 * i - 96, 1) for i in range(4)]
    out = plus[0] - minus[0]
    for i in range(1, 4):
        out = jnp.where(block == i, plus[i] - minus[i], out)
    return out


def force_kernel(
    disp_hbm, vel_hbm, lame_hbm, props_hbm, slots_hbm,
    f_out, xe_out, xo_out, abuf_hbm,
    gx, gy, sj, xs, disp, vel, lame, props, slots, abuf, sem_in, sem_out,
):
    grp = lax.axis_index("grp")
    blk = lax.axis_index("blk")
    pairs = [(disp_hbm.at[0], disp.at[0]), (lame_hbm, lame)]
    pairs += [(disp_hbm.at[1], disp.at[1]), (disp_hbm.at[2], disp.at[2])]
    pairs += [(props_hbm, props), (slots_hbm, slots)]
    pairs += [(vel_hbm.at[0], vel.at[0]), (vel_hbm.at[2], vel.at[1])]
    loads = [pltpu.make_async_copy(a, b, sem_in.at[t]) for t, (a, b) in enumerate(pairs)]
    for load in loads:
        load.start()
    lane, sub, jl, k, i_el = tile_iota()
    x0, x4, z0, z4 = own_scales(grp, blk)
    xs[...] = jnp.zeros((128, 128), F32)
    abuf[...] = jnp.zeros((640, 128), F32)
    loads[0].wait()

    for c in range(3):
        if c:
            loads[1 + c].wait()
        for r in range(5):
            u = [[row(disp, c, node(p, q, r)) for q in range(5)] for p in range(5)]
            for q in range(5):
                out = line(D_TABLE, [u[p][q] for p in range(5)])
                for p in range(5):
                    gx[c, node(p, q, r)] = out[p]
            for p in range(5):
                out = line(D_TABLE, u[p])
                for q in range(5):
                    gy[c, node(p, q, r)] = out[q]

    loads[4].wait()
    loads[5].wait()
    theta, a, b, length, pre_x, pre_z, sigma = (props[:, i, :] for i in range(7))
    xs[0:25] = pre_x
    xs[25:50] = pre_z
    xs[50:75] = 0.5 * jnp.exp((FRICTION_REF + b * jnp.log(theta / length)) / a)
    xs[75:100] = sigma * a
    packed = lax.dot_general(
        slot_hot(slots[...]), xs[...], (((1,), (1,)), ((), ())),
        precision=HIGHEST, preferred_element_type=F32,
    )
    for u in range(4):
        for i in range(4):
            t = u * 4 + i
            abuf[pl.ds(u * 160 + grp * 40 + i, 8, stride=5), :] = packed[8 * t : 8 * t + 8]

    loads[1].wait()
    lam = lame[0, :].reshape(8, 128)
    mu = lame[1, :].reshape(8, 128)
    mu2 = mu + mu
    for p in range(5):
        for q in range(5):
            gz = [
                line(D_TABLE, [row(disp, c, node(p, q, r)) for r in range(5)]) for c in range(3)
            ]
            sz = [[None] * 5 for _ in range(3)]
            for r in range(5):
                n = node(p, q, r)
                g0 = [gx[c, n] for c in range(3)]
                g1 = [gy[c, n] for c in range(3)]
                g2 = [gz[c][r] for c in range(3)]
                spread = lam * (g0[0] + g1[1] + g2[2])
                s01 = mu * (g0[1] + g1[0])
                s02 = mu * (g0[2] + g2[0])
                s12 = mu * (g1[2] + g2[1])
                gx[0, n] = spread + mu2 * g0[0]
                gx[1, n] = s01
                gx[2, n] = s02
                gy[1, n] = spread + mu2 * g1[1]
                gy[2, n] = s12
                sz[0][r], sz[1][r], sz[2][r] = s02, s12, spread + mu2 * g2[2]
            for c in range(3):
                out = line(M_TABLE, sz[c])
                for r in range(5):
                    f_out[c, node(p, q, r)] = out[r]

    y4_in, y0_in = jl < 3, jl > 0
    x4_in, x0_in = i_el < 3, i_el > 0
    z4_in, z0_in = k < 31, k > 0
    zero = jnp.zeros((8, 128), F32)

    def xy_parts(c, r):
        f = [[f_out[c, node(p, q, r)] for q in range(5)] for p in range(5)]
        for p in range(5):
            if c == 0:
                s = [gx[1, node(p, q, r)] for q in range(5)]
            else:
                s = [gy[c, node(p, q, r)] for q in range(5)]
            out = line(M_TABLE, s)
            for q in range(5):
                f[p][q] = f[p][q] + out[q]
        for q in range(5):
            out = line(M_TABLE, [gx[c, node(p, q, r)] for p in range(5)])
            for p in range(5):
                f[p][q] = f[p][q] + out[p]
        for p in range(5):
            up, down = roll(f[p][0], -32, 1), roll(f[p][4], 32, 1)
            f[p][0], f[p][4] = (
                jnp.where(y0_in, 0.5 * (f[p][0] + down), f[p][0]),
                jnp.where(y4_in, 0.5 * (f[p][4] + up), f[p][4]),
            )
        for q in range(5):
            avg = 0.5 * (f[4][q] + roll(f[0][q], -2, 0))
            f[0][q] = jnp.where(x0_in, roll(avg, 2, 0), f[0][q] * x0)
            f[4][q] = jnp.where(x4_in, avg, f[4][q] * x4)
        for p in range(5):
            for q in range(5):
                f_out[c, node(p, q, r)] = f[p][q]

    for c in range(3):
        xy_parts(c, 0)
        xy_parts(c, 4)
        for p in range(5):
            for q in range(5):
                n0, n4 = node(p, q, 0), node(p, q, 4)
                a0, a4 = f_out[c, n0], f_out[c, n4]
                up, down = roll(a0, -1, 1), roll(a4, 1, 1)
                f_out[c, n0] = jnp.where(z0_in, 0.5 * (a0 + down), a0 * z0)
                f_out[c, n4] = jnp.where(z4_in, 0.5 * (a4 + up), a4 * z4)
        for r in (1, 2, 3):
            xy_parts(c, r)

    loads[6].wait()
    loads[7].wait()
    own_x = {0: jnp.where(x0_in, 1.0, x0), 4: jnp.where(x4_in, 1.0, x4)}
    own_z = {0: jnp.where(z0_in, 1.0, z0), 4: jnp.where(z4_in, 1.0, z4)}
    odd_sub = sub % 2 == 1
    for p in range(5):
        for cc in range(2):
            c = 2 * cc
            at = 6 * (2 * p + cc)
            sides = [None] * 5
            for r in range(5):
                own = None
                for part in (own_x.get(p), own_z.get(r)):
                    if part is not None:
                        own = part if own is None else own * part
                n0, n4 = node(p, 0, r), node(p, 4, r)
                v = jnp.where(odd_sub, row(vel, cc, n0), row(vel, cc, n4))
                f = jnp.where(odd_sub, f_out[c, n0], f_out[c, n4])
                sides[r] = f + (v if own is None else v * own)
                sj[pl.ds(8 * (at + r), 8), :] = sides[r]
            extra = jnp.where(k == 0, roll(sides[4], -31, 1), 0.0)
            extra = jnp.where(k == 31, roll(sides[0], 31, 1), extra)
            sj[pl.ds(8 * (at + 5), 8), :] = extra
    for t in range(60, 64):
        sj[pl.ds(8 * t, 8), :] = zero
    y = fault_lanes(sj, 64)
    yt = jnp.concatenate([y, jnp.zeros((64, 128), F32)]).T
    dest = blk // 8
    lane32 = lax.broadcasted_iota(jnp.int32, (32, 128), 1)
    tails = [roll(yt[32 * i : 32 * i + 32], 68, 1) for i in range(4)]
    heads = yt[0:32]
    for i in range(1, 4):
        heads = jnp.where(lane32 // 32 == i, roll(yt[32 * i : 32 * i + 32], 32 * i, 1), heads)

    def put_jump(d):
        for i in range(4):
            rows = pl.ds(d * 160 + i, 32, stride=5)
            abuf[rows, :] = jnp.where(lane32 >= 100, tails[i], abuf[rows, :])
        abuf[pl.ds(d * 160 + 4, 32, stride=5), :] = heads

    put_jump(dest)

    @pl.when((blk % 8 == 7) & (dest < N_GRP - 1))
    def _():
        put_jump(dest + 1)

    @pl.when((blk % 8 == 0) & (dest > 0))
    def _():
        put_jump(dest - 1)

    stores = []
    for t in range(4):
        rows = pl.ds(160 * t, 160)
        stores.append(pltpu.make_async_copy(abuf.at[rows], abuf_hbm.at[rows], sem_out.at[t]))
    for copy in stores:
        copy.start()

    x_even = blk % 2 == 0
    for c in range(3):
        for q in range(5):
            for r in range(5):
                m = c * 25 + q * 5 + r
                lo = f_out[c, node(0, q, r)]
                hi = roll(f_out[c, node(4, q, r)], 2, 0)
                xe_out[m] = jnp.where(x_even, hi, lo)[0:2]
                xo_out[m] = jnp.where(x_even, lo, hi)[0:2]
    for copy in stores:
        copy.wait()


def middle_kernel(f_in, vel_hbm, xe, xo, p_out, ze_out, zo_out, vel, sem):
    grp = lax.axis_index("grp")
    blk = lax.axis_index("blk")
    lane, sub, jl, k, i_el = tile_iota()
    loads = [pltpu.make_async_copy(vel_hbm.at[c], vel.at[c], sem.at[c]) for c in range(3)]
    for load in loads:
        load.start()
    x_even = blk % 2 == 0
    for c in range(3):
        for n in range(125):
            p_out[c, n] = f_in[c, n]
        for q in range(5):
            for r in range(5):
                m = c * 25 + q * 5 + r
                ev, od = xe[m], xo[m]
                lo, hi = node(0, q, r), node(4, q, r)
                p_out[c, lo, 0:2] = p_out[c, lo, 0:2] + jnp.where(x_even, od, ev)
                p_out[c, hi, 6:8] = p_out[c, hi, 6:8] + jnp.where(x_even, ev, od)
    z_even = grp % 2 == 0
    for g in range(3):
        zlo = zhi = jnp.zeros((8, 128), F32)
        for m in range(32 * g, min(75, 32 * g + 32)):
            c, pq = m // 25, m % 25
            at = k == m % 32
            zlo = jnp.where(at, roll(p_out[c, 5 * pq], m % 32, 1), zlo)
            zhi = jnp.where(at, roll(p_out[c, 5 * pq + 4], m % 32 - 31, 1), zhi)
        ze_out[g] = jnp.where(z_even, zhi, zlo)
        zo_out[g] = jnp.where(z_even, zlo, zhi)
    for c in range(3):
        loads[c].wait()
        for n in range(125):
            p_out[c, n] = p_out[c, n] + row(vel, c, n)


def halo_kernel(p_in, ze, zo, p_out, jump_out, sj):
    grp = lax.axis_index("grp")
    lane, sub, jl, k, i_el = tile_iota()
    z_even = grp % 2 == 0
    zlo = [jnp.where(z_even, zo[g], ze[g]) for g in range(3)]
    zhi = [jnp.where(z_even, ze[g], zo[g]) for g in range(3)]
    for c in range(3):
        for p in range(5):
            for q in range(5):
                m = c * 25 + p * 5 + q
                n0, n4 = node(p, q, 0), node(p, q, 4)
                add0 = roll(zlo[m // 32], -(m % 32), 1)
                add4 = roll(zhi[m // 32], 31 - m % 32, 1)
                p_out[c, n0] = p_in[c, n0] + jnp.where(k == 0, add0, 0.0)
                p_out[c, n4] = p_in[c, n4] + jnp.where(k == 31, add4, 0.0)
                for r in (1, 2, 3):
                    p_out[c, node(p, q, r)] = p_in[c, node(p, q, r)]
    odd_sub = sub % 2 == 1
    for c in range(3):
        for p in range(5):
            for r in range(5):
                sj[pl.ds(8 * (c * 32 + p * 5 + r), 8), :] = jnp.where(
                    odd_sub, p_out[c, node(p, 0, r)], p_out[c, node(p, 4, r)]
                )
        for t in range(25, 32):
            sj[pl.ds(8 * (c * 32 + t), 8), :] = jnp.zeros((8, 128), F32)
    jump_out[...] = fault_lanes(sj, 96)


def solve(trial_x, trial_z, scale_c, sigma_a):
    trial_norm = jnp.sqrt(trial_x * trial_x + trial_z * trial_z)
    rate = jnp.zeros_like(trial_norm)
    for _ in range(NEWTON):
        arg = scale_c * rate
        residual = trial_norm - ETA * rate - sigma_a * inverse_sinh(arg)
        slope = -ETA - sigma_a * scale_c / jnp.sqrt(1.0 + arg * arg)
        rate = rate - residual / slope
    return trial_norm, rate


def final_kernel(
    p_in, jump, ain, props, slots,
    v_hbm, rate_out, theta_out,
    sb, xs, ys, jp, v_out, sem,
):
    grp = lax.axis_index("grp")
    blk = lax.axis_index("blk")
    lane, sub, jl, k, i_el = tile_iota()

    for i in range(4):
        ys[pl.ds(32 * i, 32), :] = ain[pl.ds(blk // 8 * 160 + i, 32, stride=5), :]
    ys[...] = ys[...].T
    t0x, t0z, scale_c, sigma_a = (ys[pl.ds(25 * j, 32), :] for j in range(4))
    trial_x = t0x + ETA * jump[0:32]
    trial_z = t0z + ETA * jump[64:96]
    trial_norm, rate = solve(trial_x, trial_z, scale_c, sigma_a)
    keep = 1.0 - ETA * rate / jnp.maximum(trial_norm, TRACTION_FLOOR)
    push = (
        CORRECTION * (trial_x * keep - t0x),
        CORRECTION * ETA * jump[32:64],
        CORRECTION * (trial_z * keep - t0z),
    )
    for c in range(3):
        for i in range(4):
            sb[pl.ds(c * 256 + 2 * i + 1, 32, stride=8), :] = roll(push[c], -32 * i, 1)
            sb[pl.ds(c * 256 + 2 * i, 32, stride=8), :] = roll(push[c], 96 - 32 * i, 1)
    plus_at = (sub % 2 == 1) & (lane < 32)
    minus_at = (sub % 2 == 0) & (lane >= 96)
    stores = []
    for c in range(3):
        for p in range(5):
            for r in range(5):
                n0, n4 = node(p, 0, r), node(p, 4, r)
                push_back = sb[pl.ds(8 * (c * 32 + p * 5 + r), 8), :]
                v_out[c, n0, :] = (p_in[c, n0] - jnp.where(plus_at, push_back, 0.0)).reshape(1024)
                v_out[c, n4, :] = (p_in[c, n4] + jnp.where(minus_at, push_back, 0.0)).reshape(1024)
                for q in (1, 2, 3):
                    v_out[c, node(p, q, r), :] = p_in[c, node(p, q, r)].reshape(1024)
        stores.append(pltpu.make_async_copy(v_out.at[c], v_hbm.at[c], sem.at[c]))
        stores[c].start()

    for u in range(4):
        heads = ain[pl.ds(u * 160 + grp * 40 + 4, 8, stride=5), :]
        for i in range(4):
            tails = roll(ain[pl.ds(u * 160 + grp * 40 + i, 8, stride=5), :], 60, 1)
            both = jnp.where(lane < 32, roll(heads, -32 * i, 1), tails)
            ys[pl.ds(8 * (u * 4 + i), 8), :] = jnp.where(lane < 60, both, 0.0)
    xs[...] = jnp.zeros((128, 128), F32)
    lane4 = lax.broadcasted_iota(jnp.int32, (4, 128), 1)
    for step, there, i, into in ((-1, grp > 0, 3, 0), (8, grp < N_GRP - 1, 0, 31)):
        first_row = jnp.where(there, (grp * 8 + step) * 5, 0)
        tails = roll(ain[pl.ds(first_row + i, 4, stride=160), :], 60, 1)
        heads = roll(ain[pl.ds(first_row + 4, 4, stride=160), :], -32 * i, 1)
        both = jnp.where(lane4 < 32, heads, tails)
        xs[pl.ds(into, 4, stride=32), :] = jnp.where((lane4 < 60) & there, both, 0.0)
    ys[...] = ys[...].T
    xs[...] = xs[...].T
    first = jnp.where(grp_is(blk, 0), 1.0, 0.0).astype(F32)
    last = jnp.where(grp_is(blk, N_BLK - 1), 1.0, 0.0).astype(F32)

    def along_z(mat, p, c):
        t = mat[pl.ds(6 * (2 * p + c // 2), 8), :]
        low = jnp.where((sub == 0) & (lane >= 32), roll(roll(t, 32, 1), -5, 0), 0.0)
        high = jnp.where((sub == 4) & (lane < 96), roll(roll(t, -32, 1), -1, 0), 0.0)
        return t + low * first + high * last

    i_at, s_at = lane // 8 % 4, lane % 8
    for c in (0, 2):
        t = [along_z(ys, p, c) for p in range(5)]
        end0, end4 = along_z(xs, 0, c), along_z(xs, 4, c)
        left = jnp.where(s_at == 0, end4, roll(t[4], -23, 1))
        right = jnp.where(s_at == 7, end0, roll(t[0], 23, 1))
        t[0], t[4] = (
            t[0] + jnp.where(i_at == 0, left, 0.0),
            t[4] + jnp.where(i_at == 3, right, 0.0),
        )
        for p in range(5):
            jp[c // 2, 5 * p : 5 * p + 5, :] = t[p][0:5]
    hot = slot_hot(slots[...])
    slot_jump = [
        lax.dot_general(
            jp[c], hot, (((1,), (0,)), ((), ())), precision=HIGHEST, preferred_element_type=F32
        )[0:25]
        for c in range(2)
    ]
    theta, a, b, length, pre_x, pre_z, sigma = (props[:, i, :] for i in range(7))
    scale_c = 0.5 * jnp.exp((FRICTION_REF + b * jnp.log(theta / length)) / a)
    _, rate = solve(
        pre_x + ETA * slot_jump[0], pre_z + ETA * slot_jump[1], scale_c, sigma * a
    )
    rate_out[...] = rate
    theta_out[...] = theta + DT * (1.0 - rate * theta / length)
    for copy in stores:
        copy.wait()


def grp_is(index, value):
    return index == value


VMEM_LIMIT = 24 << 20


def shape(*dims):
    return jax.ShapeDtypeStruct(dims, F32)


def vmem(*dims):
    return pltpu.VMEM(dims, F32)


HBM = pl.BlockSpec(memory_space=pltpu.HBM)
WHOLE = pl.BlockSpec(memory_space=pltpu.VMEM)


PARAMS = pltpu.CompilerParams(vmem_limit_bytes=VMEM_LIMIT)
FIELD = (3, 125, 8, 128)


def in_hbm(x):
    return pltpu.with_memory_space_constraint(x, pltpu.HBM)


def force_call(*args):
    return pl.pallas_call(
        force_kernel,
        name="force",
        in_specs=[HBM] * 5,
        out_specs=[WHOLE] * 3 + [HBM],
        out_shape=(
            shape(*FIELD), shape(75, 2, 128), shape(75, 2, 128), pltpu.HBM((640, 128), F32),
        ),
        scratch_shapes=[
            vmem(*FIELD), vmem(*FIELD), vmem(512, 128), vmem(128, 128),
            vmem(3, 125, 1024), vmem(2, 125, 1024), vmem(2, 1024),
            vmem(25, 7, 128), pltpu.VMEM((1, 128), jnp.int32), vmem(640, 128),
            pltpu.SemaphoreType.DMA((8,)), pltpu.SemaphoreType.DMA((4,)),
        ],
        compiler_params=PARAMS,
    )(*[in_hbm(x) for x in args])


def on_device(displacement, velocity, lame, fault_props, fault_slots):
    slots = fault_slots.reshape(1, 128)
    fault_props = jnp.transpose(fault_props, (1, 0, 2))
    even_b = [(i, i ^ 1) for i in range(N_BLK)]
    odd_b = [(i, ((i + 1) ^ 1) - 1) for i in range(1, N_BLK - 1)]
    even_g = [(i, i ^ 1) for i in range(N_GRP)]
    odd_g = [(i, ((i + 1) ^ 1) - 1) for i in range(1, N_GRP - 1)]
    f, xe, xo, abuf = force_call(displacement, velocity, lame, fault_props, slots)
    ain = lax.all_to_all(abuf.reshape(640, 1, 128), ("grp", "blk"), 0, 0, tiled=True)
    ain = ain.reshape(640, 128)
    xe = lax.ppermute(xe, "blk", even_b)
    xo = lax.ppermute(xo, "blk", odd_b)
    p, ze, zo = pl.pallas_call(
        middle_kernel,
        name="middle",
        in_specs=[WHOLE, HBM, WHOLE, WHOLE],
        out_specs=[WHOLE] * 3,
        out_shape=(shape(*FIELD), shape(3, 8, 128), shape(3, 8, 128)),
        scratch_shapes=[vmem(3, 125, 1024), pltpu.SemaphoreType.DMA((3,))],
        compiler_params=PARAMS,
    )(f, in_hbm(velocity), xe, xo)
    ze = lax.ppermute(ze, "grp", even_g)
    zo = lax.ppermute(zo, "grp", odd_g)
    p, jump = pl.pallas_call(
        halo_kernel,
        name="halo",
        in_specs=[WHOLE] * 3,
        out_specs=[WHOLE] * 2,
        out_shape=(shape(*FIELD), shape(96, 128)),
        scratch_shapes=[vmem(768, 128)],
        compiler_params=PARAMS,
    )(p, ze, zo)
    return pl.pallas_call(
        final_kernel,
        name="final",
        in_specs=[WHOLE] * 5,
        out_specs=[HBM, WHOLE, WHOLE],
        out_shape=(pltpu.HBM((3, 125, 1024), F32), shape(25, 128), shape(25, 128)),
        scratch_shapes=[
            vmem(768, 128), vmem(128, 128), vmem(128, 128), vmem(2, 32, 128),
            vmem(3, 125, 1024), pltpu.SemaphoreType.DMA((3,)),
        ],
        compiler_params=PARAMS,
    )(p, jump, ain, fault_props, slots)


def solution(mesh):
    both = ("grp", "blk")
    return jax.shard_map(
        on_device,
        mesh=mesh,
        in_specs=(P(None, None, both), P(None, None, both), P(None, both), P(None, None, both), P(both)),
        out_specs=(P(None, None, both), P(None, both), P(None, both)),
        check_vma=False,
    )
```

time: 41.7 us -> 35.9 us (0.86)
  the two profiles are of different devices: /device:TPU:1 before, /device:TPU:48 now
where the time goes in v2:
time: 35.9 us; the launch traced here: 35.7 us
  starting transfers between devices  17.9 us (50%)
  Pallas kernels  9.94 us (28%)
  waiting for transfers between devices  7.11 us (20%)
  between operations  0.72 us (2%)
    all_to_all x1, starting transfers between devices, on_device(): lax.all_to_all(abuf.reshape(640, 1, 128), ('grp', 'blk'), 0, 0, tiled=True)  10.1 us
    pallas_call x1, Pallas kernels, force_call(): pl.pallas_call(force_kernel, name='force', in_specs=[HBM] * 5, out_specs=...  5.21 us
    ppermute x1, starting transfers between devices, on_device(): xo = lax.ppermute(xo, 'blk', odd_b)  4.34 us
    ppermute x1, waiting for transfers between devices, on_device(): xo = lax.ppermute(xo, 'blk', odd_b)  3.44 us
    ppermute x1, waiting for transfers between devices, on_device(): zo = lax.ppermute(zo, 'grp', odd_g)  3.12 us
    pallas_call x1, Pallas kernels, on_device(): pl.pallas_call(final_kernel, name='final', in_specs=[WHOLE] * 5, out_spec...  2.69 us
    ppermute x1, starting transfers between devices, on_device(): zo = lax.ppermute(zo, 'grp', odd_g)  1.91 us
    pallas_call x1, Pallas kernels, on_device(): pl.pallas_call(middle_kernel, name='middle', in_specs=[WHOLE, HBM, WHOLE,...  1.66 us
  transfers between devices with their start and end apart: 5, of which 3 were waited for; matrix products, arithmetic and copies ran while one was open for 0% of the time, Pallas kernels for 6%

profile of v2, /device:TPU:48, one launch (start us, length us, event | category | flops | bytes accessed | tf_op | source)
XLA Modules:
  0.0 35.7 jit_solution(16600891304285332298)
XLA Ops:
  0.6 5.2 %force.1 = (f32[3,125,8,128]{3,2,1,0:T(8,128)S(1)}, f32[75,2,128]{2,1,0:T(2,128)S(1)}, f32[75,2,128]{2,1,0:T(2,128)S(1)}, f32[640,128]{1,0:T(8,128)}) custom-call(f32[3,125,1024]{2,1,0:T(8,128)} %disp_hbm.1, f32[3,125,1024]{2,1,0:T(8,128)} %vel_hbm.3, f32[2,1024]{1,0:T(2,128)} %lame_hbm.1, f32[25,7,128]{2,1,0:T(8,128)} %bitcast.7, s32[1,128]{1,0:T(1,128)} %bitcast.9), custom_call_target="tpu_custom_call" | custom-call | tf_op jit(solution)/shard_map/force/pallas_call | solution.py:498
  5.8 10.1 %all-to-all-start = ((f32[640,1,128]{2,1,0:T(1,128)}), f32[640,1,128]{2,1,0:T(1,128)S(1)}, u32[]{:S(2)}, u32[]{:S(2)}) async-start(f32[640,1,128]{2,1,0:T(1,128)} %bitcast.11), calls=%async_computation | async-start | bytes 655360 | tf_op jit(solution)/shard_map/all_to_all | solution.py:524
  16.0 0.2 collective-permute-start
  16.2 4.3 %collective-permute-start.1 = (f32[75,2,128]{2,1,0:T(2,128)S(1)}, f32[75,2,128]{2,1,0:T(2,128)S(1)}, u32[]{:S(2)}, u32[]{:S(2)}) collective-permute-start(f32[75,2,128]{2,1,0:T(2,128)S(1)} %get-tuple-element.14), channel_id=1, source_target_pairs={{1,2},{2,1},{3,4},{4,3},{5,6},{6,5},{7,8},{8,7},{9,10},{10,9},{11,... | collective-permute-start | bytes 230408 | tf_op jit(solution)/shard_map/ppermute | solution.py:527
  20.5 0.0 collective-permute-done.xe
  20.5 3.4 %collective-permute-done.1.xo = f32[75,2,128]{2,1,0:T(2,128)S(1)} collective-permute-done((f32[75,2,128]{2,1,0:T(2,128)S(1)}, f32[75,2,128]{2,1,0:T(2,128)S(1)}, u32[]{:S(2)}, u32[]{:S(2)}) %collective-permute-start.1) | collective-permute-done | bytes 76832 | tf_op jit(solution)/shard_map/ppermute | solution.py:527
  24.0 0.0 copy-start.1
  24.0 1.7 %middle.1 = (f32[3,125,8,128]{3,2,1,0:T(8,128)S(1)}, f32[3,8,128]{2,1,0:T(8,128)S(1)}, f32[3,8,128]{2,1,0:T(8,128)S(1)}) custom-call(f32[3,125,8,128]{3,2,1,0:T(8,128)S(1)} %get-tuple-element.12.f_in, f32[3,125,1024]{2,1,0:T(8,128)} %vel_hbm.3, f32[75,2,128]{2,1,0:T(2,128)S(1)} %collective-permute-done.xe, f32[75,2,128]{2,1,0:T(2,128)S(1)} %collective-permute-done.1.xo), custom_call_target="tpu_custom_call" | custom-call | tf_op jit(solution)/shard_map/middle/pallas_call | solution.py:528
  25.7 0.0 copy-start
  25.7 1.3 %collective-permute-start.2 = (f32[3,8,128]{2,1,0:T(8,128)S(1)}, f32[3,8,128]{2,1,0:T(8,128)S(1)}, u32[]{:S(2)}, u32[]{:S(2)}) collective-permute-start(f32[3,8,128]{2,1,0:T(8,128)S(1)} %get-tuple-element.16), channel_id=1, source_target_pairs={{0,32},{32,0},{64,96},{96,64},{1,33},{33,1},{65,97},{97,65},{2,34}... | collective-permute-start | bytes 36872 | tf_op jit(solution)/shard_map/ppermute | solution.py:537
  27.0 1.9 %collective-permute-start.3 = (f32[3,8,128]{2,1,0:T(8,128)S(1)}, f32[3,8,128]{2,1,0:T(8,128)S(1)}, u32[]{:S(2)}, u32[]{:S(2)}) collective-permute-start(f32[3,8,128]{2,1,0:T(8,128)S(1)} %get-tuple-element.17), channel_id=1, source_target_pairs={{32,64},{64,32},{33,65},{65,33},{34,66},{66,34},{35,67},{67,35},{3... | collective-permute-start | bytes 36872 | tf_op jit(solution)/shard_map/ppermute | solution.py:538
  28.9 0.5 %collective-permute-done.2.ze = f32[3,8,128]{2,1,0:T(8,128)S(1)} collective-permute-done((f32[3,8,128]{2,1,0:T(8,128)S(1)}, f32[3,8,128]{2,1,0:T(8,128)S(1)}, u32[]{:S(2)}, u32[]{:S(2)}) %collective-permute-start.2) | collective-permute-done | bytes 12320 | tf_op jit(solution)/shard_map/ppermute | solution.py:537
  29.4 3.1 %collective-permute-done.3.zo = f32[3,8,128]{2,1,0:T(8,128)S(1)} collective-permute-done((f32[3,8,128]{2,1,0:T(8,128)S(1)}, f32[3,8,128]{2,1,0:T(8,128)S(1)}, u32[]{:S(2)}, u32[]{:S(2)}) %collective-permute-start.3) | collective-permute-done | bytes 12320 | tf_op jit(solution)/shard_map/ppermute | solution.py:538
  32.6 0.4 %halo.1 = (f32[3,125,8,128]{3,2,1,0:T(8,128)S(1)}, f32[96,128]{1,0:T(8,128)S(1)}) custom-call(f32[3,125,8,128]{3,2,1,0:T(8,128)S(1)} %get-tuple-element.15.p_in, f32[3,8,128]{2,1,0:T(8,128)S(1)} %collective-permute-done.2.ze, f32[3,8,128]{2,1,0:T(8,128)S(1)} %collective-permute-done.3.zo), custom_call_target="tpu_custom_call" | custom-call | tf_op jit(solution)/shard_map/halo/pallas_call | solution.py:539
  33.0 0.0 all-to-all-done
  33.0 0.0 copy-done.1
  33.0 0.0 copy-done
  33.0 2.7 %final.1 = (f32[3,125,1024]{2,1,0:T(8,128)}, f32[25,128]{1,0:T(8,128)}, f32[25,128]{1,0:T(8,128)}) custom-call(f32[3,125,8,128]{3,2,1,0:T(8,128)S(1)} %get-tuple-element.18.p_in, f32[96,128]{1,0:T(8,128)S(1)} %get-tuple-element.19.jump, f32[640,128]{1,0:T(8,128)S(1)} %bitcast.6, f32[25,7,128]{2,1,0:T(8,128)S(1)} %bitcast.8, s32[1,128]{1,0:T(1,128)S(1)} %bitcast.10), custom_call_target="tpu_custom_call" | custom-call | tf_op jit(solution)/shard_map/final/pallas_call | solution.py:548
Async XLA Ops:
  5.8 27.1 %all-to-all-start = ((f32[640,1,128]{2,1,0:T(1,128)}), f32[640,1,128]{2,1,0:T(1,128)S(1)}, u32[]{:S(2)}, u32[]{:S(2)}) async-start(f32[640,1,128]{2,1,0:T(1,128)} %bitcast.11), calls=%async_computation | async-start | bytes 655360 | tf_op jit(solution)/shard_map/all_to_all | solution.py:524
  16.0 4.6 %collective-permute-start = (f32[75,2,128]{2,1,0:T(2,128)S(1)}, f32[75,2,128]{2,1,0:T(2,128)S(1)}, u32[]{:S(2)}, u32[]{:S(2)}) collective-permute-start(f32[75,2,128]{2,1,0:T(2,128)S(1)} %get-tuple-element.13), channel_id=1, source_target_pairs={{0,1},{1,0},{2,3},{3,2},{4,5},{5,4},{6,7},{7,6},{8,9},{9,8},{10,11... | collective-permute-start | bytes 230408 | tf_op jit(solution)/shard_map/ppermute | solution.py:526
  16.2 7.8 %collective-permute-start.1 = (f32[75,2,128]{2,1,0:T(2,128)S(1)}, f32[75,2,128]{2,1,0:T(2,128)S(1)}, u32[]{:S(2)}, u32[]{:S(2)}) collective-permute-start(f32[75,2,128]{2,1,0:T(2,128)S(1)} %get-tuple-element.14), channel_id=1, source_target_pairs={{1,2},{2,1},{3,4},{4,3},{5,6},{6,5},{7,8},{8,7},{9,10},{10,9},{11,... | collective-permute-start | bytes 230408 | tf_op jit(solution)/shard_map/ppermute | solution.py:527
  24.0 9.0 %copy-start.1 = (s32[128]{0:T(128)S(1)}, s32[128]{0:T(128)}, u32[]{:S(2)}) copy-start(s32[128]{0:T(128)} %param.9) | copy-start | bytes 1540
  25.7 7.3 %copy-start = (f32[7,25,128]{2,0,1:T(8,128)S(1)}, f32[7,25,128]{2,0,1:T(8,128)}, u32[]{:S(2)}) copy-start(f32[7,25,128]{2,0,1:T(8,128)} %param.8) | copy-start | bytes 268804
  25.7 3.8 %collective-permute-start.2 = (f32[3,8,128]{2,1,0:T(8,128)S(1)}, f32[3,8,128]{2,1,0:T(8,128)S(1)}, u32[]{:S(2)}, u32[]{:S(2)}) collective-permute-start(f32[3,8,128]{2,1,0:T(8,128)S(1)} %get-tuple-element.16), channel_id=1, source_target_pairs={{0,32},{32,0},{64,96},{96,64},{1,33},{33,1},{65,97},{97,65},{2,34}... | collective-permute-start | bytes 36872 | tf_op jit(solution)/shard_map/ppermute | solution.py:537
  27.0 5.6 %collective-permute-start.3 = (f32[3,8,128]{2,1,0:T(8,128)S(1)}, f32[3,8,128]{2,1,0:T(8,128)S(1)}, u32[]{:S(2)}, u32[]{:S(2)}) collective-permute-start(f32[3,8,128]{2,1,0:T(8,128)S(1)} %get-tuple-element.17), channel_id=1, source_target_pairs={{32,64},{64,32},{33,65},{65,33},{34,66},{66,34},{35,67},{67,35},{3... | collective-permute-start | bytes 36872 | tf_op jit(solution)/shard_map/ppermute | solution.py:538

commit v3 on v2

--- a/solution.py
+++ b/solution.py
@@ -103,7 +103,7 @@
 
 def force_kernel(
     disp_hbm, vel_hbm, lame_hbm, props_hbm, slots_hbm,
-    f_out, xe_out, xo_out, abuf_hbm,
+    f_out, xe_out, xo_out, ze_out, zo_out, abuf_hbm,
     gx, gy, sj, xs, disp, vel, lame, props, slots, abuf, sem_in, sem_out,
 ):
     grp = lax.axis_index("grp")
@@ -118,7 +118,7 @@
     lane, sub, jl, k, i_el = tile_iota()
     x0, x4, z0, z4 = own_scales(grp, blk)
     xs[...] = jnp.zeros((128, 128), F32)
-    abuf[...] = jnp.zeros((640, 128), F32)
+    abuf[...] = jnp.zeros((768, 128), F32)
     loads[0].wait()
 
     for c in range(3):
@@ -149,7 +149,7 @@
     for u in range(4):
         for i in range(4):
             t = u * 4 + i
-            abuf[pl.ds(u * 160 + grp * 40 + i, 8, stride=5), :] = packed[8 * t : 8 * t + 8]
+            abuf[pl.ds(u * 192 + grp * 48 + i, 8, stride=6), :] = packed[8 * t : 8 * t + 8]
 
     loads[1].wait()
     lam = lame[0, :].reshape(8, 128)
@@ -263,9 +263,9 @@
 
     def put_jump(d):
         for i in range(4):
-            rows = pl.ds(d * 160 + i, 32, stride=5)
+            rows = pl.ds(d * 192 + i, 32, stride=6)
             abuf[rows, :] = jnp.where(lane32 >= 100, tails[i], abuf[rows, :])
-        abuf[pl.ds(d * 160 + 4, 32, stride=5), :] = heads
+        abuf[pl.ds(d * 192 + 4, 32, stride=6), :] = heads
 
     put_jump(dest)
 
@@ -277,9 +277,25 @@
     def _():
         put_jump(dest - 1)
 
+    for dg in (-1, 1):
+        edge = zero
+        for m in range(15):
+            c, q = m // 5, m % 5
+            r = 4 if dg > 0 else 0
+            value = jnp.where(sub < 4, f_out[c, node(0, q, r)], f_out[c, node(4, q, r)])
+            edge = jnp.where(k == m, roll(value, m - (31 if dg > 0 else 0), 1), edge)
+        edge = jnp.where(k < 15, edge, roll(roll(edge, 15, 1), -1, 0))
+        for db, at in ((-1, 0), (1, 6)):
+            to_g, to_b = grp + dg, blk + db
+            there = (to_g >= 0) & (to_g < N_GRP) & (to_b >= 0) & (to_b < N_BLK)
+
+            @pl.when(there)
+            def _(edge=edge, at=at, to_g=to_g, to_b=to_b):
+                abuf[pl.ds(6 * (to_g * N_BLK + to_b) + 5, 1), :] = edge[at : at + 1]
+
     stores = []
     for t in range(4):
-        rows = pl.ds(160 * t, 160)
+        rows = pl.ds(192 * t, 192)
         stores.append(pltpu.make_async_copy(abuf.at[rows], abuf_hbm.at[rows], sem_out.at[t]))
     for copy in stores:
         copy.start()
@@ -293,11 +309,22 @@
                 hi = roll(f_out[c, node(4, q, r)], 2, 0)
                 xe_out[m] = jnp.where(x_even, hi, lo)[0:2]
                 xo_out[m] = jnp.where(x_even, lo, hi)[0:2]
+
+    z_even = grp % 2 == 0
+    for g in range(3):
+        zlo = zhi = jnp.zeros((8, 128), F32)
+        for m in range(32 * g, min(75, 32 * g + 32)):
+            c, pq = m // 25, m % 25
+            at = k == m % 32
+            zlo = jnp.where(at, roll(f_out[c, 5 * pq], m % 32, 1), zlo)
+            zhi = jnp.where(at, roll(f_out[c, 5 * pq + 4], m % 32 - 31, 1), zhi)
+        ze_out[g] = jnp.where(z_even, zhi, zlo)
+        zo_out[g] = jnp.where(z_even, zlo, zhi)
     for copy in stores:
         copy.wait()
 
 
-def middle_kernel(f_in, vel_hbm, xe, xo, p_out, ze_out, zo_out, vel, sem):
+def halo_kernel(f_in, vel_hbm, xe, xo, ze, zo, p_out, vel, sem):
     grp = lax.axis_index("grp")
     blk = lax.axis_index("blk")
     lane, sub, jl, k, i_el = tile_iota()
@@ -305,9 +332,24 @@
     for load in loads:
         load.start()
     x_even = blk % 2 == 0
-    for c in range(3):
-        for n in range(125):
-            p_out[c, n] = f_in[c, n]
+    z_even = grp % 2 == 0
+    zlo = [jnp.where(z_even, zo[g], ze[g]) for g in range(3)]
+    zhi = [jnp.where(z_even, ze[g], zo[g]) for g in range(3)]
+    for c in range(3):
+        loads[c].wait()
+        for p in range(5):
+            for q in range(5):
+                m = c * 25 + p * 5 + q
+                add0 = roll(zlo[m // 32], -(m % 32), 1)
+                add4 = roll(zhi[m // 32], 31 - m % 32, 1)
+                for r in range(5):
+                    n = node(p, q, r)
+                    value = f_in[c, n] + row(vel, c, n)
+                    if r == 0:
+                        value = value + jnp.where(k == 0, add0, 0.0)
+                    if r == 4:
+                        value = value + jnp.where(k == 31, add4, 0.0)
+                    p_out[c, n] = value
         for q in range(5):
             for r in range(5):
                 m = c * 25 + q * 5 + r
@@ -315,49 +357,6 @@
                 lo, hi = node(0, q, r), node(4, q, r)
                 p_out[c, lo, 0:2] = p_out[c, lo, 0:2] + jnp.where(x_even, od, ev)
                 p_out[c, hi, 6:8] = p_out[c, hi, 6:8] + jnp.where(x_even, ev, od)
-    z_even = grp % 2 == 0
-    for g in range(3):
-        zlo = zhi = jnp.zeros((8, 128), F32)
-        for m in range(32 * g, min(75, 32 * g + 32)):
-            c, pq = m // 25, m % 25
-            at = k == m % 32
-            zlo = jnp.where(at, roll(p_out[c, 5 * pq], m % 32, 1), zlo)
-            zhi = jnp.where(at, roll(p_out[c, 5 * pq + 4], m % 32 - 31, 1), zhi)
-        ze_out[g] = jnp.where(z_even, zhi, zlo)
-        zo_out[g] = jnp.where(z_even, zlo, zhi)
-    for c in range(3):
-        loads[c].wait()
-        for n in range(125):
-            p_out[c, n] = p_out[c, n] + row(vel, c, n)
-
-
-def halo_kernel(p_in, ze, zo, p_out, jump_out, sj):
-    grp = lax.axis_index("grp")
-    lane, sub, jl, k, i_el = tile_iota()
-    z_even = grp % 2 == 0
-    zlo = [jnp.where(z_even, zo[g], ze[g]) for g in range(3)]
-    zhi = [jnp.where(z_even, ze[g], zo[g]) for g in range(3)]
-    for c in range(3):
-        for p in range(5):
-            for q in range(5):
-                m = c * 25 + p * 5 + q
-                n0, n4 = node(p, q, 0), node(p, q, 4)
-                add0 = roll(zlo[m // 32], -(m % 32), 1)
-                add4 = roll(zhi[m // 32], 31 - m % 32, 1)
-                p_out[c, n0] = p_in[c, n0] + jnp.where(k == 0, add0, 0.0)
-                p_out[c, n4] = p_in[c, n4] + jnp.where(k == 31, add4, 0.0)
-                for r in (1, 2, 3):
-                    p_out[c, node(p, q, r)] = p_in[c, node(p, q, r)]
-    odd_sub = sub % 2 == 1
-    for c in range(3):
-        for p in range(5):
-            for r in range(5):
-                sj[pl.ds(8 * (c * 32 + p * 5 + r), 8), :] = jnp.where(
-                    odd_sub, p_out[c, node(p, 0, r)], p_out[c, node(p, 4, r)]
-                )
-        for t in range(25, 32):
-            sj[pl.ds(8 * (c * 32 + t), 8), :] = jnp.zeros((8, 128), F32)
-    jump_out[...] = fault_lanes(sj, 96)
 
 
 def solve(trial_x, trial_z, scale_c, sigma_a):
@@ -372,16 +371,48 @@
 
 
 def final_kernel(
-    p_in, jump, ain, props, slots,
+    p_in, ain, props, slots,
     v_hbm, rate_out, theta_out,
-    sb, xs, ys, jp, v_out, sem,
+    sj, xs, ys, jp, v_out, er, sem,
 ):
     grp = lax.axis_index("grp")
     blk = lax.axis_index("blk")
     lane, sub, jl, k, i_el = tile_iota()
 
+    for dg in (-1, 1):
+        both = None
+        for db in (-1, 1):
+            from_g, from_b = grp + dg, blk + db
+            there = (from_g >= 0) & (from_g < N_GRP) & (from_b >= 0) & (from_b < N_BLK)
+            at = jnp.where(there, 6 * (from_g * N_BLK + from_b) + 5, 0)
+            value = jnp.broadcast_to(ain[pl.ds(at, 1), :], (8, 128))
+            value = jnp.where(there, jnp.where(sub % 2 == 0, value, roll(value, -15, 1)), 0.0)
+            both = value if both is None else jnp.where(sub < 4, both, value)
+        kept = jnp.where((sub < 2) | (sub >= 6), both, 0.0)
+        to = 31 if dg > 0 else 0
+        for m in range(15):
+            er[(dg + 1) // 2, m] = jnp.where(k == to, roll(kept, to - m, 1), 0.0)
+
+    def field(c, p, q, r):
+        value = p_in[c, node(p, q, r)]
+        if p in (0, 4) and r in (0, 4):
+            edge = er[r // 4, c * 5 + q]
+            value = value + jnp.where((sub < 4) == (p == 0), edge, 0.0)
+        return value
+
+    odd_sub = sub % 2 == 1
+    for c in range(3):
+        for p in range(5):
+            for r in range(5):
+                sj[pl.ds(8 * (c * 32 + p * 5 + r), 8), :] = jnp.where(
+                    odd_sub, field(c, p, 0, r), field(c, p, 4, r)
+                )
+        for t in range(25, 32):
+            sj[pl.ds(8 * (c * 32 + t), 8), :] = jnp.zeros((8, 128), F32)
+    jump = fault_lanes(sj, 96)
+    sb = sj
     for i in range(4):
-        ys[pl.ds(32 * i, 32), :] = ain[pl.ds(blk // 8 * 160 + i, 32, stride=5), :]
+        ys[pl.ds(32 * i, 32), :] = ain[pl.ds(blk // 8 * 192 + i, 32, stride=6), :]
     ys[...] = ys[...].T
     t0x, t0z, scale_c, sigma_a = (ys[pl.ds(25 * j, 32), :] for j in range(4))
     trial_x = t0x + ETA * jump[0:32]
@@ -405,25 +436,25 @@
             for r in range(5):
                 n0, n4 = node(p, 0, r), node(p, 4, r)
                 push_back = sb[pl.ds(8 * (c * 32 + p * 5 + r), 8), :]
-                v_out[c, n0, :] = (p_in[c, n0] - jnp.where(plus_at, push_back, 0.0)).reshape(1024)
-                v_out[c, n4, :] = (p_in[c, n4] + jnp.where(minus_at, push_back, 0.0)).reshape(1024)
+                v_out[c, n0, :] = (field(c, p, 0, r) - jnp.where(plus_at, push_back, 0.0)).reshape(1024)
+                v_out[c, n4, :] = (field(c, p, 4, r) + jnp.where(minus_at, push_back, 0.0)).reshape(1024)
                 for q in (1, 2, 3):
-                    v_out[c, node(p, q, r), :] = p_in[c, node(p, q, r)].reshape(1024)
+                    v_out[c, node(p, q, r), :] = field(c, p, q, r).reshape(1024)
         stores.append(pltpu.make_async_copy(v_out.at[c], v_hbm.at[c], sem.at[c]))
         stores[c].start()
 
     for u in range(4):
-        heads = ain[pl.ds(u * 160 + grp * 40 + 4, 8, stride=5), :]
+        heads = ain[pl.ds(u * 192 + grp * 48 + 4, 8, stride=6), :]
         for i in range(4):
-            tails = roll(ain[pl.ds(u * 160 + grp * 40 + i, 8, stride=5), :], 60, 1)
+            tails = roll(ain[pl.ds(u * 192 + grp * 48 + i, 8, stride=6), :], 60, 1)
             both = jnp.where(lane < 32, roll(heads, -32 * i, 1), tails)
             ys[pl.ds(8 * (u * 4 + i), 8), :] = jnp.where(lane < 60, both, 0.0)
     xs[...] = jnp.zeros((128, 128), F32)
     lane4 = lax.broadcasted_iota(jnp.int32, (4, 128), 1)
     for step, there, i, into in ((-1, grp > 0, 3, 0), (8, grp < N_GRP - 1, 0, 31)):
-        first_row = jnp.where(there, (grp * 8 + step) * 5, 0)
-        tails = roll(ain[pl.ds(first_row + i, 4, stride=160), :], 60, 1)
-        heads = roll(ain[pl.ds(first_row + 4, 4, stride=160), :], -32 * i, 1)
+        first_row = jnp.where(there, (grp * 8 + step) * 6, 0)
+        tails = roll(ain[pl.ds(first_row + i, 4, stride=192), :], 60, 1)
+        heads = roll(ain[pl.ds(first_row + 4, 4, stride=192), :], -32 * i, 1)
         both = jnp.where(lane4 < 32, heads, tails)
         xs[pl.ds(into, 4, stride=32), :] = jnp.where((lane4 < 60) & there, both, 0.0)
     ys[...] = ys[...].T
@@ -499,14 +530,15 @@
         force_kernel,
         name="force",
         in_specs=[HBM] * 5,
-        out_specs=[WHOLE] * 3 + [HBM],
+        out_specs=[WHOLE] * 5 + [HBM],
         out_shape=(
-            shape(*FIELD), shape(75, 2, 128), shape(75, 2, 128), pltpu.HBM((640, 128), F32),
+            shape(*FIELD), shape(75, 2, 128), shape(75, 2, 128),
+            shape(3, 8, 128), shape(3, 8, 128), pltpu.HBM((768, 128), F32),
         ),
         scratch_shapes=[
             vmem(*FIELD), vmem(*FIELD), vmem(512, 128), vmem(128, 128),
             vmem(3, 125, 1024), vmem(2, 125, 1024), vmem(2, 1024),
-            vmem(25, 7, 128), pltpu.VMEM((1, 128), jnp.int32), vmem(640, 128),
+            vmem(25, 7, 128), pltpu.VMEM((1, 128), jnp.int32), vmem(768, 128),
             pltpu.SemaphoreType.DMA((8,)), pltpu.SemaphoreType.DMA((4,)),
         ],
         compiler_params=PARAMS,
@@ -520,43 +552,34 @@
     odd_b = [(i, ((i + 1) ^ 1) - 1) for i in range(1, N_BLK - 1)]
     even_g = [(i, i ^ 1) for i in range(N_GRP)]
     odd_g = [(i, ((i + 1) ^ 1) - 1) for i in range(1, N_GRP - 1)]
-    f, xe, xo, abuf = force_call(displacement, velocity, lame, fault_props, slots)
-    ain = lax.all_to_all(abuf.reshape(640, 1, 128), ("grp", "blk"), 0, 0, tiled=True)
-    ain = ain.reshape(640, 128)
+    f, xe, xo, ze, zo, abuf = force_call(displacement, velocity, lame, fault_props, slots)
+    ain = lax.all_to_all(abuf.reshape(768, 1, 128), ("grp", "blk"), 0, 0, tiled=True)
+    ain = ain.reshape(768, 128)
     xe = lax.ppermute(xe, "blk", even_b)
     xo = lax.ppermute(xo, "blk", odd_b)
-    p, ze, zo = pl.pallas_call(
-        middle_kernel,
-        name="middle",
-        in_specs=[WHOLE, HBM, WHOLE, WHOLE],
-        out_specs=[WHOLE] * 3,
-        out_shape=(shape(*FIELD), shape(3, 8, 128), shape(3, 8, 128)),
+    ze = lax.ppermute(ze, "grp", even_g)
+    zo = lax.ppermute(zo, "grp", odd_g)
+    p = pl.pallas_call(
+        halo_kernel,
+        name="halo",
+        in_specs=[WHOLE, HBM] + [WHOLE] * 4,
+        out_specs=WHOLE,
+        out_shape=shape(*FIELD),
         scratch_shapes=[vmem(3, 125, 1024), pltpu.SemaphoreType.DMA((3,))],
         compiler_params=PARAMS,
-    )(f, in_hbm(velocity), xe, xo)
-    ze = lax.ppermute(ze, "grp", even_g)
-    zo = lax.ppermute(zo, "grp", odd_g)
-    p, jump = pl.pallas_call(
-        halo_kernel,
-        name="halo",
-        in_specs=[WHOLE] * 3,
-        out_specs=[WHOLE] * 2,
-        out_shape=(shape(*FIELD), shape(96, 128)),
-        scratch_shapes=[vmem(768, 128)],
-        compiler_params=PARAMS,
-    )(p, ze, zo)
+    )(f, in_hbm(velocity), xe, xo, ze, zo)
     return pl.pallas_call(
         final_kernel,
         name="final",
-        in_specs=[WHOLE] * 5,
+        in_specs=[WHOLE] * 4,
         out_specs=[HBM, WHOLE, WHOLE],
         out_shape=(pltpu.HBM((3, 125, 1024), F32), shape(25, 128), shape(25, 128)),
         scratch_shapes=[
             vmem(768, 128), vmem(128, 128), vmem(128, 128), vmem(2, 32, 128),
-            vmem(3, 125, 1024), pltpu.SemaphoreType.DMA((3,)),
+            vmem(3, 125, 1024), vmem(2, 15, 8, 128), pltpu.SemaphoreType.DMA((3,)),
         ],
         compiler_params=PARAMS,
-    )(p, jump, ain, fault_props, slots)
+    )(p, ain, fault_props, slots)
 
 
 def solution(mesh):

time: 35.9 us -> 34.3 us (0.955)
  the two profiles are of different devices: /device:TPU:48 before, /device:TPU:1 now
where the time goes in v3:
time: 34.3 us; the launch traced here: 34.1 us
  starting transfers between devices  17.1 us (50%)
  Pallas kernels  10.4 us (30%)
  waiting for transfers between devices  4.99 us (15%)
  local copies, waits for them, and re-layouts  0.9 us (3%)
  between operations  0.68 us (2%)
    all_to_all x1, starting transfers between devices, on_device(): lax.all_to_all(abuf.reshape(768, 1, 128), ('grp', 'blk'), 0, 0, tiled=True)  11.5 us
    pallas_call x1, Pallas kernels, force_call(): pl.pallas_call(force_kernel, name='force', in_specs=[HBM] * 5, out_specs=...  5.67 us
    all_to_all x1, waiting for transfers between devices, on_device(): lax.all_to_all(abuf.reshape(768, 1, 128), ('grp', 'blk'), 0, 0, tiled=True)  3.52 us
    pallas_call x1, Pallas kernels, on_device(): pl.pallas_call(final_kernel, name='final', in_specs=[WHOLE] * 4, out_spec...  3.15 us
    ppermute x1, starting transfers between devices, on_device(): xo = lax.ppermute(xo, 'blk', odd_b)  2.58 us
    pallas_call x1, Pallas kernels, on_device(): pl.pallas_call(halo_kernel, name='halo', in_specs=[WHOLE, HBM] + [WHOLE]...  1.54 us
    ppermute x1, waiting for transfers between devices, on_device(): ze = lax.ppermute(ze, 'grp', even_g)  1.41 us
    ppermute x1, starting transfers between devices, on_device(): ze = lax.ppermute(ze, 'grp', even_g)  1.27 us
  transfers between devices with their start and end apart: 5, of which 3 were waited for; matrix products, arithmetic and copies ran while one was open for 0% of the time, Pallas kernels for 5%

profile of v3, /device:TPU:1, one launch (start us, length us, event | category | flops | bytes accessed | tf_op | source)
XLA Modules:
  0.0 34.1 jit_solution(7864825989696904782)
XLA Ops:
  0.6 5.7 %force.1 = (f32[3,125,8,128]{3,2,1,0:T(8,128)S(1)}, f32[75,2,128]{2,1,0:T(2,128)S(1)}, f32[75,2,128]{2,1,0:T(2,128)S(1)}, f32[3,8,128]{2,1,0:T(8,128)S(1)}, f32[...) custom-call(f32[3,125,1024]{2,1,0:T(8,128)} %disp_hbm.1, f32[3,125,1024]{2,1,0:T(8,128)} %vel_hbm.3, f32[2,1024]{1,0:T(2,128)} %lame_hbm.1, ...), custom_call_target="tpu_custom_call" | custom-call | tf_op jit(solution)/shard_map/force/pallas_call | solution.py:529
  6.3 11.5 %all-to-all-start = ((f32[768,1,128]{2,1,0:T(1,128)}), f32[768,1,128]{2,1,0:T(1,128)S(1)}, u32[]{:S(2)}, u32[]{:S(2)}) async-start(f32[768,1,128]{2,1,0:T(1,128)} %bitcast.11), calls=%async_computation | async-start | bytes 786432 | tf_op jit(solution)/shard_map/all_to_all | solution.py:556
  17.8 1.1 %collective-permute-start = (f32[75,2,128]{2,1,0:T(2,128)S(1)}, f32[75,2,128]{2,1,0:T(2,128)S(1)}, u32[]{:S(2)}, u32[]{:S(2)}) collective-permute-start(f32[75,2,128]{2,1,0:T(2,128)S(1)} %get-tuple-element.10), channel_id=1, source_target_pairs={{0,1},{1,0},{2,3},{3,2},{4,5},{5,4},{6,7},{7,6},{8,9},{9,8},{10,11... | collective-permute-start | bytes 230408 | tf_op jit(solution)/shard_map/ppermute | solution.py:558
  19.0 2.6 %collective-permute-start.1 = (f32[75,2,128]{2,1,0:T(2,128)S(1)}, f32[75,2,128]{2,1,0:T(2,128)S(1)}, u32[]{:S(2)}, u32[]{:S(2)}) collective-permute-start(f32[75,2,128]{2,1,0:T(2,128)S(1)} %get-tuple-element.11), channel_id=1, source_target_pairs={{1,2},{2,1},{3,4},{4,3},{5,6},{6,5},{7,8},{8,7},{9,10},{10,9},{11,... | collective-permute-start | bytes 230408 | tf_op jit(solution)/shard_map/ppermute | solution.py:559
  21.5 1.3 %collective-permute-start.2 = (f32[3,8,128]{2,1,0:T(8,128)S(1)}, f32[3,8,128]{2,1,0:T(8,128)S(1)}, u32[]{:S(2)}, u32[]{:S(2)}) collective-permute-start(f32[3,8,128]{2,1,0:T(8,128)S(1)} %get-tuple-element.12), channel_id=1, source_target_pairs={{0,32},{32,0},{64,96},{96,64},{1,33},{33,1},{65,97},{97,65},{2,34}... | collective-permute-start | bytes 36872 | tf_op jit(solution)/shard_map/ppermute | solution.py:560
  22.8 0.7 %collective-permute-start.3 = (f32[3,8,128]{2,1,0:T(8,128)S(1)}, f32[3,8,128]{2,1,0:T(8,128)S(1)}, u32[]{:S(2)}, u32[]{:S(2)}) collective-permute-start(f32[3,8,128]{2,1,0:T(8,128)S(1)} %get-tuple-element.13), channel_id=1, source_target_pairs={{32,64},{64,32},{33,65},{65,33},{34,66},{66,34},{35,67},{67,35},{3... | collective-permute-start | bytes 36872 | tf_op jit(solution)/shard_map/ppermute | solution.py:561
  23.5 1.4 %collective-permute-done.2.ze = f32[3,8,128]{2,1,0:T(8,128)S(1)} collective-permute-done((f32[3,8,128]{2,1,0:T(8,128)S(1)}, f32[3,8,128]{2,1,0:T(8,128)S(1)}, u32[]{:S(2)}, u32[]{:S(2)}) %collective-permute-start.2) | collective-permute-done | bytes 12320 | tf_op jit(solution)/shard_map/ppermute | solution.py:560
  24.9 0.0 collective-permute-done.3.zo
  24.9 0.0 collective-permute-done.xe
  24.9 0.1 collective-permute-done.1.xo
  24.9 0.0 copy-start.1
  24.9 1.5 %halo.1.p_in = f32[3,125,8,128]{3,2,1,0:T(8,128)S(1)} custom-call(f32[3,125,8,128]{3,2,1,0:T(8,128)S(1)} %get-tuple-element.9.f_in, f32[3,125,1024]{2,1,0:T(8,128)} %vel_hbm.3, f32[75,2,128]{2,1,0:T(2,128)S(1)} %collective-permute-done.xe, f32[75,2,128]{2,1,0:T(2,128)S(1)} %collective-permute-done.1.xo, f32[3,8,128]{2,1,0:T(8,128)S(1)} %collective-permute-done.2.ze, ...), custom_call_target="tpu_custom_call" | custom-call | tf_op jit(solution)/shard_map/halo/pallas_call | solution.py:562
  26.5 3.5 %all-to-all-done = f32[768,1,128]{2,1,0:T(1,128)S(1)} async-done(((f32[768,1,128]{2,1,0:T(1,128)}), f32[768,1,128]{2,1,0:T(1,128)S(1)}, u32[]{:S(2)}, u32[]{:S(2)}) %all-to-all-start) | async-done | bytes 393248 | tf_op jit(solution)/shard_map/all_to_all | solution.py:556
  30.0 0.0 copy-done.1
  30.0 0.0 copy-start
  30.0 0.9 %copy-done = f32[7,25,128]{2,0,1:T(8,128)S(1)} copy-done((f32[7,25,128]{2,0,1:T(8,128)S(1)}, f32[7,25,128]{2,0,1:T(8,128)}, u32[]{:S(2)}) %copy-start) | copy-done | bytes 89624
  30.9 3.1 %final.1 = (f32[3,125,1024]{2,1,0:T(8,128)}, f32[25,128]{1,0:T(8,128)}, f32[25,128]{1,0:T(8,128)}) custom-call(f32[3,125,8,128]{3,2,1,0:T(8,128)S(1)} %halo.1.p_in, f32[768,128]{1,0:T(8,128)S(1)} %bitcast.6, f32[25,7,128]{2,1,0:T(8,128)S(1)} %bitcast.8, s32[1,128]{1,0:T(1,128)S(1)} %bitcast.10), custom_call_target="tpu_custom_call" | custom-call | tf_op jit(solution)/shard_map/final/pallas_call | solution.py:571
Async XLA Ops:
  6.3 23.7 %all-to-all-start = ((f32[768,1,128]{2,1,0:T(1,128)}), f32[768,1,128]{2,1,0:T(1,128)S(1)}, u32[]{:S(2)}, u32[]{:S(2)}) async-start(f32[768,1,128]{2,1,0:T(1,128)} %bitcast.11), calls=%async_computation | async-start | bytes 786432 | tf_op jit(solution)/shard_map/all_to_all | solution.py:556
  17.8 7.1 %collective-permute-start = (f32[75,2,128]{2,1,0:T(2,128)S(1)}, f32[75,2,128]{2,1,0:T(2,128)S(1)}, u32[]{:S(2)}, u32[]{:S(2)}) collective-permute-start(f32[75,2,128]{2,1,0:T(2,128)S(1)} %get-tuple-element.10), channel_id=1, source_target_pairs={{0,1},{1,0},{2,3},{3,2},{4,5},{5,4},{6,7},{7,6},{8,9},{9,8},{10,11... | collective-permute-start | bytes 230408 | tf_op jit(solution)/shard_map/ppermute | solution.py:558
  19.0 6.0 %collective-permute-start.1 = (f32[75,2,128]{2,1,0:T(2,128)S(1)}, f32[75,2,128]{2,1,0:T(2,128)S(1)}, u32[]{:S(2)}, u32[]{:S(2)}) collective-permute-start(f32[75,2,128]{2,1,0:T(2,128)S(1)} %get-tuple-element.11), channel_id=1, source_target_pairs={{1,2},{2,1},{3,4},{4,3},{5,6},{6,5},{7,8},{8,7},{9,10},{10,9},{11,... | collective-permute-start | bytes 230408 | tf_op jit(solution)/shard_map/ppermute | solution.py:559
  21.5 3.3 %collective-permute-start.2 = (f32[3,8,128]{2,1,0:T(8,128)S(1)}, f32[3,8,128]{2,1,0:T(8,128)S(1)}, u32[]{:S(2)}, u32[]{:S(2)}) collective-permute-start(f32[3,8,128]{2,1,0:T(8,128)S(1)} %get-tuple-element.12), channel_id=1, source_target_pairs={{0,32},{32,0},{64,96},{96,64},{1,33},{33,1},{65,97},{97,65},{2,34}... | collective-permute-start | bytes 36872 | tf_op jit(solution)/shard_map/ppermute | solution.py:560
  22.8 2.1 %collective-permute-start.3 = (f32[3,8,128]{2,1,0:T(8,128)S(1)}, f32[3,8,128]{2,1,0:T(8,128)S(1)}, u32[]{:S(2)}, u32[]{:S(2)}) collective-permute-start(f32[3,8,128]{2,1,0:T(8,128)S(1)} %get-tuple-element.13), channel_id=1, source_target_pairs={{32,64},{64,32},{33,65},{65,33},{34,66},{66,34},{35,67},{67,35},{3... | collective-permute-start | bytes 36872 | tf_op jit(solution)/shard_map/ppermute | solution.py:561
  24.9 5.1 %copy-start.1 = (s32[128]{0:T(128)S(1)}, s32[128]{0:T(128)}, u32[]{:S(2)}) copy-start(s32[128]{0:T(128)} %param.9) | copy-start | bytes 1540
  30.0 0.9 %copy-start = (f32[7,25,128]{2,0,1:T(8,128)S(1)}, f32[7,25,128]{2,0,1:T(8,128)}, u32[]{:S(2)}) copy-start(f32[7,25,128]{2,0,1:T(8,128)} %param.8) | copy-start | bytes 268804

commit v4 on v3

--- a/solution.py
+++ b/solution.py
@@ -113,7 +113,7 @@
     pairs += [(props_hbm, props), (slots_hbm, slots)]
     pairs += [(vel_hbm.at[0], vel.at[0]), (vel_hbm.at[2], vel.at[1])]
     loads = [pltpu.make_async_copy(a, b, sem_in.at[t]) for t, (a, b) in enumerate(pairs)]
-    for load in loads:
+    for load in loads[:6]:
         load.start()
     lane, sub, jl, k, i_el = tile_iota()
     x0, x4, z0, z4 = own_scales(grp, blk)
@@ -124,6 +124,9 @@
     for c in range(3):
         if c:
             loads[1 + c].wait()
+        if c == 2:
+            loads[6].start()
+            loads[7].start()
         for r in range(5):
             u = [[row(disp, c, node(p, q, r)) for q in range(5)] for p in range(5)]
             for q in range(5):
@@ -214,7 +217,7 @@
             for q in range(5):
                 f_out[c, node(p, q, r)] = f[p][q]
 
-    for c in range(3):
+    def assemble(c):
         xy_parts(c, 0)
         xy_parts(c, 4)
         for p in range(5):
@@ -226,6 +229,9 @@
                 f_out[c, n4] = jnp.where(z4_in, 0.5 * (a4 + up), a4 * z4)
         for r in (1, 2, 3):
             xy_parts(c, r)
+
+    assemble(0)
+    assemble(2)
 
     loads[6].wait()
     loads[7].wait()
@@ -254,6 +260,7 @@
         sj[pl.ds(8 * t, 8), :] = zero
     y = fault_lanes(sj, 64)
     yt = jnp.concatenate([y, jnp.zeros((64, 128), F32)]).T
+    assemble(1)
     dest = blk // 8
     lane32 = lax.broadcasted_iota(jnp.int32, (32, 128), 1)
     tails = [roll(yt[32 * i : 32 * i + 32], 68, 1) for i in range(4)]
@@ -371,12 +378,16 @@
 
 
 def final_kernel(
-    p_in, ain, props, slots,
+    p_in, ain, props_hbm, slots_hbm,
     v_hbm, rate_out, theta_out,
-    sj, xs, ys, jp, v_out, er, sem,
+    sj, xs, ys, jp, v_out, er, props, slots, sem, sem_in,
 ):
     grp = lax.axis_index("grp")
     blk = lax.axis_index("blk")
+    pairs = ((props_hbm, props), (slots_hbm, slots))
+    loads = [pltpu.make_async_copy(a, b, sem_in.at[t]) for t, (a, b) in enumerate(pairs)]
+    for load in loads:
+        load.start()
     lane, sub, jl, k, i_el = tile_iota()
 
     for dg in (-1, 1):
@@ -480,6 +491,8 @@
         )
         for p in range(5):
             jp[c // 2, 5 * p : 5 * p + 5, :] = t[p][0:5]
+    for load in loads:
+        load.wait()
     hot = slot_hot(slots[...])
     slot_jump = [
         lax.dot_general(
@@ -571,15 +584,17 @@
     return pl.pallas_call(
         final_kernel,
         name="final",
-        in_specs=[WHOLE] * 4,
+        in_specs=[WHOLE, WHOLE, HBM, HBM],
         out_specs=[HBM, WHOLE, WHOLE],
         out_shape=(pltpu.HBM((3, 125, 1024), F32), shape(25, 128), shape(25, 128)),
         scratch_shapes=[
             vmem(768, 128), vmem(128, 128), vmem(128, 128), vmem(2, 32, 128),
-            vmem(3, 125, 1024), vmem(2, 15, 8, 128), pltpu.SemaphoreType.DMA((3,)),
+            vmem(3, 125, 1024), vmem(2, 15, 8, 128), vmem(25, 7, 128),
+            pltpu.VMEM((1, 128), jnp.int32), pltpu.SemaphoreType.DMA((3,)),
+            pltpu.SemaphoreType.DMA((2,)),
         ],
         compiler_params=PARAMS,
-    )(p, ain, fault_props, slots)
+    )(p, ain, in_hbm(fault_props), in_hbm(slots))
 
 
 def solution(mesh):

time: 34.3 us -> 33 us (0.962)
  local copies, waits for them, and re-layouts: 0.9 us -> 0 us
  Pallas kernels: 10.4 us -> 9.95 us
    unnamed x4 -> x0, local copies, waits for them, and re-layouts: 0.9 us -> none
where the time goes in v4:
time: 33 us; the launch traced here: 32.8 us
  starting transfers between devices  17.1 us (52%)
  Pallas kernels  9.95 us (30%)
  waiting for transfers between devices  5.01 us (15%)
  between operations  0.67 us (2%)
    all_to_all x1, starting transfers between devices, on_device(): lax.all_to_all(abuf.reshape(768, 1, 128), ('grp', 'blk'), 0, 0, tiled=True)  11.5 us
    pallas_call x1, Pallas kernels, force_call(): pl.pallas_call(force_kernel, name='force', in_specs=[HBM] * 5, out_specs=...  5.55 us
    all_to_all x1, waiting for transfers between devices, on_device(): lax.all_to_all(abuf.reshape(768, 1, 128), ('grp', 'blk'), 0, 0, tiled=True)  3.53 us
    pallas_call x1, Pallas kernels, on_device(): pl.pallas_call(final_kernel, name='final', in_specs=[WHOLE, WHOLE, HBM, H...  2.87 us
    ppermute x1, starting transfers between devices, on_device(): xo = lax.ppermute(xo, 'blk', odd_b)  2.58 us
    pallas_call x1, Pallas kernels, on_device(): pl.pallas_call(halo_kernel, name='halo', in_specs=[WHOLE, HBM] + [WHOLE]...  1.53 us
    ppermute x1, waiting for transfers between devices, on_device(): ze = lax.ppermute(ze, 'grp', even_g)  1.41 us
    ppermute x1, starting transfers between devices, on_device(): ze = lax.ppermute(ze, 'grp', even_g)  1.27 us
  transfers between devices with their start and end apart: 5, of which 3 were waited for; matrix products, arithmetic and copies ran while one was open for 0% of the time, Pallas kernels for 5%

profile of v4, /device:TPU:1, one launch (start us, length us, event | category | flops | bytes accessed | tf_op | source)
XLA Modules:
  0.0 32.8 jit_solution(7925792547531235680)
XLA Ops:
  0.6 5.6 %force.1 = (f32[3,125,8,128]{3,2,1,0:T(8,128)S(1)}, f32[75,2,128]{2,1,0:T(2,128)S(1)}, f32[75,2,128]{2,1,0:T(2,128)S(1)}, f32[3,8,128]{2,1,0:T(8,128)S(1)}, f32[...) custom-call(f32[3,125,1024]{2,1,0:T(8,128)} %disp_hbm.1, f32[3,125,1024]{2,1,0:T(8,128)} %vel_hbm.3, f32[2,1024]{1,0:T(2,128)} %lame_hbm.1, ...), custom_call_target="tpu_custom_call" | custom-call | tf_op jit(solution)/shard_map/force/pallas_call | solution.py:542
  6.2 11.5 %all-to-all-start = ((f32[768,1,128]{2,1,0:T(1,128)}), f32[768,1,128]{2,1,0:T(1,128)S(1)}, u32[]{:S(2)}, u32[]{:S(2)}) async-start(f32[768,1,128]{2,1,0:T(1,128)} %bitcast.9), calls=%async_computation | async-start | bytes 786432 | tf_op jit(solution)/shard_map/all_to_all | solution.py:569
  17.7 1.1 %collective-permute-start = (f32[75,2,128]{2,1,0:T(2,128)S(1)}, f32[75,2,128]{2,1,0:T(2,128)S(1)}, u32[]{:S(2)}, u32[]{:S(2)}) collective-permute-start(f32[75,2,128]{2,1,0:T(2,128)S(1)} %get-tuple-element.10), channel_id=1, source_target_pairs={{0,1},{1,0},{2,3},{3,2},{4,5},{5,4},{6,7},{7,6},{8,9},{9,8},{10,11... | collective-permute-start | bytes 230408 | tf_op jit(solution)/shard_map/ppermute | solution.py:571
  18.8 2.6 %collective-permute-start.1 = (f32[75,2,128]{2,1,0:T(2,128)S(1)}, f32[75,2,128]{2,1,0:T(2,128)S(1)}, u32[]{:S(2)}, u32[]{:S(2)}) collective-permute-start(f32[75,2,128]{2,1,0:T(2,128)S(1)} %get-tuple-element.11), channel_id=1, source_target_pairs={{1,2},{2,1},{3,4},{4,3},{5,6},{6,5},{7,8},{8,7},{9,10},{10,9},{11,... | collective-permute-start | bytes 230408 | tf_op jit(solution)/shard_map/ppermute | solution.py:572
  21.4 1.3 %collective-permute-start.2 = (f32[3,8,128]{2,1,0:T(8,128)S(1)}, f32[3,8,128]{2,1,0:T(8,128)S(1)}, u32[]{:S(2)}, u32[]{:S(2)}) collective-permute-start(f32[3,8,128]{2,1,0:T(8,128)S(1)} %get-tuple-element.12), channel_id=1, source_target_pairs={{0,32},{32,0},{64,96},{96,64},{1,33},{33,1},{65,97},{97,65},{2,34}... | collective-permute-start | bytes 36872 | tf_op jit(solution)/shard_map/ppermute | solution.py:573
  22.7 0.7 %collective-permute-start.3 = (f32[3,8,128]{2,1,0:T(8,128)S(1)}, f32[3,8,128]{2,1,0:T(8,128)S(1)}, u32[]{:S(2)}, u32[]{:S(2)}) collective-permute-start(f32[3,8,128]{2,1,0:T(8,128)S(1)} %get-tuple-element.13), channel_id=1, source_target_pairs={{32,64},{64,32},{33,65},{65,33},{34,66},{66,34},{35,67},{67,35},{3... | collective-permute-start | bytes 36872 | tf_op jit(solution)/shard_map/ppermute | solution.py:574
  23.3 1.4 %collective-permute-done.2.ze = f32[3,8,128]{2,1,0:T(8,128)S(1)} collective-permute-done((f32[3,8,128]{2,1,0:T(8,128)S(1)}, f32[3,8,128]{2,1,0:T(8,128)S(1)}, u32[]{:S(2)}, u32[]{:S(2)}) %collective-permute-start.2) | collective-permute-done | bytes 12320 | tf_op jit(solution)/shard_map/ppermute | solution.py:573
  24.8 0.0 collective-permute-done.3.zo
  24.8 0.0 collective-permute-done.xe
  24.8 0.1 collective-permute-done.1.xo
  24.8 1.5 %halo.1.p_in = f32[3,125,8,128]{3,2,1,0:T(8,128)S(1)} custom-call(f32[3,125,8,128]{3,2,1,0:T(8,128)S(1)} %get-tuple-element.9.f_in, f32[3,125,1024]{2,1,0:T(8,128)} %vel_hbm.3, f32[75,2,128]{2,1,0:T(2,128)S(1)} %collective-permute-done.xe, f32[75,2,128]{2,1,0:T(2,128)S(1)} %collective-permute-done.1.xo, f32[3,8,128]{2,1,0:T(8,128)S(1)} %collective-permute-done.2.ze, ...), custom_call_target="tpu_custom_call" | custom-call | tf_op jit(solution)/shard_map/halo/pallas_call | solution.py:575
  26.4 3.5 %all-to-all-done = f32[768,1,128]{2,1,0:T(1,128)S(1)} async-done(((f32[768,1,128]{2,1,0:T(1,128)}), f32[768,1,128]{2,1,0:T(1,128)S(1)}, u32[]{:S(2)}, u32[]{:S(2)}) %all-to-all-start) | async-done | bytes 393248 | tf_op jit(solution)/shard_map/all_to_all | solution.py:569
  29.9 2.9 %final.1 = (f32[3,125,1024]{2,1,0:T(8,128)}, f32[25,128]{1,0:T(8,128)}, f32[25,128]{1,0:T(8,128)}) custom-call(f32[3,125,8,128]{3,2,1,0:T(8,128)S(1)} %halo.1.p_in, f32[768,128]{1,0:T(8,128)S(1)} %bitcast.6, f32[25,7,128]{2,1,0:T(8,128)} %bitcast.8, s32[1,128]{1,0:T(1,128)} %bitcast.11), custom_call_target="tpu_custom_call" | custom-call | tf_op jit(solution)/shard_map/final/pallas_call | solution.py:584
Async XLA Ops:
  6.2 23.7 %all-to-all-start = ((f32[768,1,128]{2,1,0:T(1,128)}), f32[768,1,128]{2,1,0:T(1,128)S(1)}, u32[]{:S(2)}, u32[]{:S(2)}) async-start(f32[768,1,128]{2,1,0:T(1,128)} %bitcast.9), calls=%async_computation | async-start | bytes 786432 | tf_op jit(solution)/shard_map/all_to_all | solution.py:569
  17.7 7.1 %collective-permute-start = (f32[75,2,128]{2,1,0:T(2,128)S(1)}, f32[75,2,128]{2,1,0:T(2,128)S(1)}, u32[]{:S(2)}, u32[]{:S(2)}) collective-permute-start(f32[75,2,128]{2,1,0:T(2,128)S(1)} %get-tuple-element.10), channel_id=1, source_target_pairs={{0,1},{1,0},{2,3},{3,2},{4,5},{5,4},{6,7},{7,6},{8,9},{9,8},{10,11... | collective-permute-start | bytes 230408 | tf_op jit(solution)/shard_map/ppermute | solution.py:571
  18.8 6.0 %collective-permute-start.1 = (f32[75,2,128]{2,1,0:T(2,128)S(1)}, f32[75,2,128]{2,1,0:T(2,128)S(1)}, u32[]{:S(2)}, u32[]{:S(2)}) collective-permute-start(f32[75,2,128]{2,1,0:T(2,128)S(1)} %get-tuple-element.11), channel_id=1, source_target_pairs={{1,2},{2,1},{3,4},{4,3},{5,6},{6,5},{7,8},{8,7},{9,10},{10,9},{11,... | collective-permute-start | bytes 230408 | tf_op jit(solution)/shard_map/ppermute | solution.py:572
  21.4 3.3 %collective-permute-start.2 = (f32[3,8,128]{2,1,0:T(8,128)S(1)}, f32[3,8,128]{2,1,0:T(8,128)S(1)}, u32[]{:S(2)}, u32[]{:S(2)}) collective-permute-start(f32[3,8,128]{2,1,0:T(8,128)S(1)} %get-tuple-element.12), channel_id=1, source_target_pairs={{0,32},{32,0},{64,96},{96,64},{1,33},{33,1},{65,97},{97,65},{2,34}... | collective-permute-start | bytes 36872 | tf_op jit(solution)/shard_map/ppermute | solution.py:573
  22.7 2.1 %collective-permute-start.3 = (f32[3,8,128]{2,1,0:T(8,128)S(1)}, f32[3,8,128]{2,1,0:T(8,128)S(1)}, u32[]{:S(2)}, u32[]{:S(2)}) collective-permute-start(f32[3,8,128]{2,1,0:T(8,128)S(1)} %get-tuple-element.13), channel_id=1, source_target_pairs={{32,64},{64,32},{33,65},{65,33},{34,66},{66,34},{35,67},{67,35},{3... | collective-permute-start | bytes 36872 | tf_op jit(solution)/shard_map/ppermute | solution.py:574

commit v5 on v4

--- a/solution.py
+++ b/solution.py
@@ -261,29 +261,6 @@
     y = fault_lanes(sj, 64)
     yt = jnp.concatenate([y, jnp.zeros((64, 128), F32)]).T
     assemble(1)
-    dest = blk // 8
-    lane32 = lax.broadcasted_iota(jnp.int32, (32, 128), 1)
-    tails = [roll(yt[32 * i : 32 * i + 32], 68, 1) for i in range(4)]
-    heads = yt[0:32]
-    for i in range(1, 4):
-        heads = jnp.where(lane32 // 32 == i, roll(yt[32 * i : 32 * i + 32], 32 * i, 1), heads)
-
-    def put_jump(d):
-        for i in range(4):
-            rows = pl.ds(d * 192 + i, 32, stride=6)
-            abuf[rows, :] = jnp.where(lane32 >= 100, tails[i], abuf[rows, :])
-        abuf[pl.ds(d * 192 + 4, 32, stride=6), :] = heads
-
-    put_jump(dest)
-
-    @pl.when((blk % 8 == 7) & (dest < N_GRP - 1))
-    def _():
-        put_jump(dest + 1)
-
-    @pl.when((blk % 8 == 0) & (dest > 0))
-    def _():
-        put_jump(dest - 1)
-
     for dg in (-1, 1):
         edge = zero
         for m in range(15):
@@ -299,6 +276,29 @@
             @pl.when(there)
             def _(edge=edge, at=at, to_g=to_g, to_b=to_b):
                 abuf[pl.ds(6 * (to_g * N_BLK + to_b) + 5, 1), :] = edge[at : at + 1]
+
+    dest = blk // 8
+    lane32 = lax.broadcasted_iota(jnp.int32, (32, 128), 1)
+    tails = [roll(yt[32 * i : 32 * i + 32], 68, 1) for i in range(4)]
+    heads = yt[0:32]
+    for i in range(1, 4):
+        heads = jnp.where(lane32 // 32 == i, roll(yt[32 * i : 32 * i + 32], 32 * i, 1), heads)
+
+    def put_jump(d):
+        for i in range(4):
+            rows = pl.ds(d * 192 + i, 32, stride=6)
+            abuf[rows, :] = jnp.where(lane32 >= 100, tails[i], abuf[rows, :])
+        abuf[pl.ds(d * 192 + 4, 32, stride=6), :] = heads
+
+    put_jump(dest)
+
+    @pl.when((blk % 8 == 7) & (dest < N_GRP - 1))
+    def _():
+        put_jump(dest + 1)
+
+    @pl.when((blk % 8 == 0) & (dest > 0))
+    def _():
+        put_jump(dest - 1)
 
     stores = []
     for t in range(4):

time: 33 us -> 33 us (level)
  no operation moved by 1% of the time
where the time goes in v5:
time: 33 us; the launch traced here: 32.7 us
  starting transfers between devices  17.1 us (52%)
  Pallas kernels  9.87 us (30%)
  waiting for transfers between devices  5.01 us (15%)
  between operations  0.67 us (2%)
    all_to_all x1, starting transfers between devices, on_device(): lax.all_to_all(abuf.reshape(768, 1, 128), ('grp', 'blk'), 0, 0, tiled=True)  11.5 us
    pallas_call x1, Pallas kernels, force_call(): pl.pallas_call(force_kernel, name='force', in_specs=[HBM] * 5, out_specs=...  5.48 us
    all_to_all x1, waiting for transfers between devices, on_device(): lax.all_to_all(abuf.reshape(768, 1, 128), ('grp', 'blk'), 0, 0, tiled=True)  3.53 us
    pallas_call x1, Pallas kernels, on_device(): pl.pallas_call(final_kernel, name='final', in_specs=[WHOLE, WHOLE, HBM, H...  2.87 us
    ppermute x1, starting transfers between devices, on_device(): xo = lax.ppermute(xo, 'blk', odd_b)  2.58 us
    pallas_call x1, Pallas kernels, on_device(): pl.pallas_call(halo_kernel, name='halo', in_specs=[WHOLE, HBM] + [WHOLE]...  1.53 us
    ppermute x1, waiting for transfers between devices, on_device(): ze = lax.ppermute(ze, 'grp', even_g)  1.41 us
    ppermute x1, starting transfers between devices, on_device(): ze = lax.ppermute(ze, 'grp', even_g)  1.27 us
  transfers between devices with their start and end apart: 5, of which 3 were waited for; matrix products, arithmetic and copies ran while one was open for 0% of the time, Pallas kernels for 5%

profile of v5, /device:TPU:1, one launch (start us, length us, event | category | flops | bytes accessed | tf_op | source)
XLA Modules:
  0.0 32.7 jit_solution(15607999080301688703)
XLA Ops:
  0.6 5.5 %force.1 = (f32[3,125,8,128]{3,2,1,0:T(8,128)S(1)}, f32[75,2,128]{2,1,0:T(2,128)S(1)}, f32[75,2,128]{2,1,0:T(2,128)S(1)}, f32[3,8,128]{2,1,0:T(8,128)S(1)}, f32[...) custom-call(f32[3,125,1024]{2,1,0:T(8,128)} %disp_hbm.1, f32[3,125,1024]{2,1,0:T(8,128)} %vel_hbm.3, f32[2,1024]{1,0:T(2,128)} %lame_hbm.1, ...), custom_call_target="tpu_custom_call" | custom-call | tf_op jit(solution)/shard_map/force/pallas_call | solution.py:542
  6.1 11.5 %all-to-all-start = ((f32[768,1,128]{2,1,0:T(1,128)}), f32[768,1,128]{2,1,0:T(1,128)S(1)}, u32[]{:S(2)}, u32[]{:S(2)}) async-start(f32[768,1,128]{2,1,0:T(1,128)} %bitcast.9), calls=%async_computation | async-start | bytes 786432 | tf_op jit(solution)/shard_map/all_to_all | solution.py:569
  17.6 1.1 %collective-permute-start = (f32[75,2,128]{2,1,0:T(2,128)S(1)}, f32[75,2,128]{2,1,0:T(2,128)S(1)}, u32[]{:S(2)}, u32[]{:S(2)}) collective-permute-start(f32[75,2,128]{2,1,0:T(2,128)S(1)} %get-tuple-element.10), channel_id=1, source_target_pairs={{0,1},{1,0},{2,3},{3,2},{4,5},{5,4},{6,7},{7,6},{8,9},{9,8},{10,11... | collective-permute-start | bytes 230408 | tf_op jit(solution)/shard_map/ppermute | solution.py:571
  18.8 2.6 %collective-permute-start.1 = (f32[75,2,128]{2,1,0:T(2,128)S(1)}, f32[75,2,128]{2,1,0:T(2,128)S(1)}, u32[]{:S(2)}, u32[]{:S(2)}) collective-permute-start(f32[75,2,128]{2,1,0:T(2,128)S(1)} %get-tuple-element.11), channel_id=1, source_target_pairs={{1,2},{2,1},{3,4},{4,3},{5,6},{6,5},{7,8},{8,7},{9,10},{10,9},{11,... | collective-permute-start | bytes 230408 | tf_op jit(solution)/shard_map/ppermute | solution.py:572
  21.3 1.3 %collective-permute-start.2 = (f32[3,8,128]{2,1,0:T(8,128)S(1)}, f32[3,8,128]{2,1,0:T(8,128)S(1)}, u32[]{:S(2)}, u32[]{:S(2)}) collective-permute-start(f32[3,8,128]{2,1,0:T(8,128)S(1)} %get-tuple-element.12), channel_id=1, source_target_pairs={{0,32},{32,0},{64,96},{96,64},{1,33},{33,1},{65,97},{97,65},{2,34}... | collective-permute-start | bytes 36872 | tf_op jit(solution)/shard_map/ppermute | solution.py:573
  22.6 0.7 %collective-permute-start.3 = (f32[3,8,128]{2,1,0:T(8,128)S(1)}, f32[3,8,128]{2,1,0:T(8,128)S(1)}, u32[]{:S(2)}, u32[]{:S(2)}) collective-permute-start(f32[3,8,128]{2,1,0:T(8,128)S(1)} %get-tuple-element.13), channel_id=1, source_target_pairs={{32,64},{64,32},{33,65},{65,33},{34,66},{66,34},{35,67},{67,35},{3... | collective-permute-start | bytes 36872 | tf_op jit(solution)/shard_map/ppermute | solution.py:574
  23.3 1.4 %collective-permute-done.2.ze = f32[3,8,128]{2,1,0:T(8,128)S(1)} collective-permute-done((f32[3,8,128]{2,1,0:T(8,128)S(1)}, f32[3,8,128]{2,1,0:T(8,128)S(1)}, u32[]{:S(2)}, u32[]{:S(2)}) %collective-permute-start.2) | collective-permute-done | bytes 12320 | tf_op jit(solution)/shard_map/ppermute | solution.py:573
  24.7 0.0 collective-permute-done.3.zo
  24.7 0.0 collective-permute-done.xe
  24.7 0.1 collective-permute-done.1.xo
  24.8 1.5 %halo.1.p_in = f32[3,125,8,128]{3,2,1,0:T(8,128)S(1)} custom-call(f32[3,125,8,128]{3,2,1,0:T(8,128)S(1)} %get-tuple-element.9.f_in, f32[3,125,1024]{2,1,0:T(8,128)} %vel_hbm.3, f32[75,2,128]{2,1,0:T(2,128)S(1)} %collective-permute-done.xe, f32[75,2,128]{2,1,0:T(2,128)S(1)} %collective-permute-done.1.xo, f32[3,8,128]{2,1,0:T(8,128)S(1)} %collective-permute-done.2.ze, ...), custom_call_target="tpu_custom_call" | custom-call | tf_op jit(solution)/shard_map/halo/pallas_call | solution.py:575
  26.3 3.5 %all-to-all-done = f32[768,1,128]{2,1,0:T(1,128)S(1)} async-done(((f32[768,1,128]{2,1,0:T(1,128)}), f32[768,1,128]{2,1,0:T(1,128)S(1)}, u32[]{:S(2)}, u32[]{:S(2)}) %all-to-all-start) | async-done | bytes 393248 | tf_op jit(solution)/shard_map/all_to_all | solution.py:569
  29.8 2.9 %final.1 = (f32[3,125,1024]{2,1,0:T(8,128)}, f32[25,128]{1,0:T(8,128)}, f32[25,128]{1,0:T(8,128)}) custom-call(f32[3,125,8,128]{3,2,1,0:T(8,128)S(1)} %halo.1.p_in, f32[768,128]{1,0:T(8,128)S(1)} %bitcast.6, f32[25,7,128]{2,1,0:T(8,128)} %bitcast.8, s32[1,128]{1,0:T(1,128)} %bitcast.11), custom_call_target="tpu_custom_call" | custom-call | tf_op jit(solution)/shard_map/final/pallas_call | solution.py:584
Async XLA Ops:
  6.1 23.7 %all-to-all-start = ((f32[768,1,128]{2,1,0:T(1,128)}), f32[768,1,128]{2,1,0:T(1,128)S(1)}, u32[]{:S(2)}, u32[]{:S(2)}) async-start(f32[768,1,128]{2,1,0:T(1,128)} %bitcast.9), calls=%async_computation | async-start | bytes 786432 | tf_op jit(solution)/shard_map/all_to_all | solution.py:569
  17.6 7.1 %collective-permute-start = (f32[75,2,128]{2,1,0:T(2,128)S(1)}, f32[75,2,128]{2,1,0:T(2,128)S(1)}, u32[]{:S(2)}, u32[]{:S(2)}) collective-permute-start(f32[75,2,128]{2,1,0:T(2,128)S(1)} %get-tuple-element.10), channel_id=1, source_target_pairs={{0,1},{1,0},{2,3},{3,2},{4,5},{5,4},{6,7},{7,6},{8,9},{9,8},{10,11... | collective-permute-start | bytes 230408 | tf_op jit(solution)/shard_map/ppermute | solution.py:571
  18.8 6.0 %collective-permute-start.1 = (f32[75,2,128]{2,1,0:T(2,128)S(1)}, f32[75,2,128]{2,1,0:T(2,128)S(1)}, u32[]{:S(2)}, u32[]{:S(2)}) collective-permute-start(f32[75,2,128]{2,1,0:T(2,128)S(1)} %get-tuple-element.11), channel_id=1, source_target_pairs={{1,2},{2,1},{3,4},{4,3},{5,6},{6,5},{7,8},{8,7},{9,10},{10,9},{11,... | collective-permute-start | bytes 230408 | tf_op jit(solution)/shard_map/ppermute | solution.py:572
  21.3 3.3 %collective-permute-start.2 = (f32[3,8,128]{2,1,0:T(8,128)S(1)}, f32[3,8,128]{2,1,0:T(8,128)S(1)}, u32[]{:S(2)}, u32[]{:S(2)}) collective-permute-start(f32[3,8,128]{2,1,0:T(8,128)S(1)} %get-tuple-element.12), channel_id=1, source_target_pairs={{0,32},{32,0},{64,96},{96,64},{1,33},{33,1},{65,97},{97,65},{2,34}... | collective-permute-start | bytes 36872 | tf_op jit(solution)/shard_map/ppermute | solution.py:573
  22.6 2.1 %collective-permute-start.3 = (f32[3,8,128]{2,1,0:T(8,128)S(1)}, f32[3,8,128]{2,1,0:T(8,128)S(1)}, u32[]{:S(2)}, u32[]{:S(2)}) collective-permute-start(f32[3,8,128]{2,1,0:T(8,128)S(1)} %get-tuple-element.13), channel_id=1, source_target_pairs={{32,64},{64,32},{33,65},{65,33},{34,66},{66,34},{35,67},{67,35},{3... | collective-permute-start | bytes 36872 | tf_op jit(solution)/shard_map/ppermute | solution.py:574
